TPU v7x, 256 devices: a whole 4x4x8 slice. The times are simulated.
256 devices in a mesh: occ: 16 (over z_hi, y, core), vir: 16 (over z_lo, x).
Axes of the slice: x: 4, y: 4, z: 8 (z_hi: 2, z_lo: 4; z = z_hi * 4 + z_lo), core: 2. Of those that a mesh axis runs over, the one named last changes fastest.
Arguments:
- amplitudes: bfloat16 [8192, 8192], P('occ', 'vir'), may hold values from -6 to 6
- hole_integrals: bfloat16 [8192, 8192], P('occ'), may hold values from -0.1875 to 0.1875
- particle_integrals: bfloat16 [8192, 8192], P('vir'), may hold values from -0.25 to 0.25
- occ_irrep: int32 [128], replicated, may hold values from 0 to 7
- vir_irrep: int32 [128], replicated, may hold values from 0 to 7
- occ_energy: float32 [8192], P('occ'), may hold values from -1.5 to -0.5
- vir_energy: float32 [8192], P('vir'), may hold values from 0.5 to 2.5
Outputs:
- update: float32 [8192, 8192], P('vir', 'occ')
All inputs are finite; a program needn't handle non-finite values.
Results may differ from a plain program's by a relative error of at most 0.0003.
Values may be sent and summed in bfloat16 or wider, within the bound.
No kernel may reach another device: no remote copies, remote signals or barrier semaphores. Data moves between devices by JAX's collectives and lax.ppermute only.
A program may use at most 128 MiB of HBM per device.

v0:
```python
import jax
import jax.numpy as jnp
from jax import lax
from jax.sharding import PartitionSpec as P

TILE = 64


def per_device(
    amplitudes, hole_integrals, particle_integrals, occ_irrep, vir_irrep, occ_energy, vir_energy
):
    own_rows = amplitudes.shape[0]
    own_pairs = amplitudes.shape[1]
    zero_value = jnp.zeros((), jnp.bfloat16)
    occ_labels = jnp.repeat(occ_irrep, TILE)
    vir_labels = jnp.repeat(vir_irrep, TILE)
    own_occ = lax.dynamic_slice_in_dim(occ_labels, lax.axis_index("occ") * own_rows, own_rows)
    own_vir = lax.dynamic_slice_in_dim(vir_labels, lax.axis_index("vir") * own_pairs, own_pairs)
    hole_masked = jnp.where(own_occ[:, None] == occ_labels[None, :], hole_integrals, zero_value)
    contract_first = (((0,), (1,)), ((), ()))
    hole = lax.dot_general(
        lax.all_gather(amplitudes, "occ", axis=0, tiled=True),
        hole_masked,
        contract_first,
        preferred_element_type=jnp.float32,
    )
    slab_masked = jnp.where(own_vir[:, None] == vir_labels[None, :], particle_integrals, zero_value)
    particle = lax.psum_scatter(
        lax.dot_general(
            slab_masked, amplitudes, contract_first, preferred_element_type=jnp.float32
        ),
        "vir",
        scatter_dimension=0,
        tiled=True,
    )
    energy_gap = vir_energy[:, None] - occ_energy[None, :]
    return (hole + particle) / energy_gap


def solution(mesh):
    placed = (P("occ", "vir"), P("occ", None), P("vir", None), P(), P(), P("occ"), P("vir"))
    return jax.shard_map(
        per_device, mesh=mesh, in_specs=placed, out_specs=P("vir", "occ"), check_vma=False
    )
```

profile of v0, /device:TPU:65, one launch (start us, length us, event | category | flops | bytes accessed | tf_op | source)
XLA Modules:
  0.0 290.1 jit_solution(7640333086408449033)
XLA Ops:
  7.4 0.0 all-gather.2.cloned.1.call-start
  7.4 0.7 all-gather.2.cloned.1.call-update
  8.1 0.0 reduce-scatter.2.cloned.1.call-start
  8.1 0.7 broadcast_in_dim.17
  8.9 0.1 reshape.13
  9.0 0.1 dynamic_slice.7
  9.0 14.0 %fusion.1 = f32[8192,512]{0,1:T(8,128)} fusion(bf16[512,512]{1,0:T(8,128)(2,1)} %param.7, bf16[512,8192]{1,0:T(8,128)(2,1)} %param.9, s32[8192]{0:T(1024)S(1)} %reshape.13, s32[512]{0:T(512)S(1)} %dynamic_slice.7), kind=kOutput, calls=%fused_computation.3 | convolution fusion | flops 4303355904 | bytes 25724928 | tf_op jit(solution)/shard_map/dot_general | solution.py:29
  23.0 0.0 copy-start
  23.0 0.0 copy-start.1
  23.0 0.0 copy-start.2
  23.0 0.0 reduce-scatter.2.cloned.1.call-update
  23.0 0.6 copy-done
  23.7 0.1 broadcast_in_dim.15
  23.7 0.1 reshape.12
  23.8 0.1 dynamic_slice.6
  23.9 246.9 %all-gather.2.cloned.1.call-done = bf16[8192,512]{1,0:T(8,128)(2,1)} async-done(((bf16[512,512]{1,0:T(8,128)(2,1)}), bf16[8192,512]{1,0:T(8,128)(2,1)}) %all-gather.2.cloned.1.call-update) | async-done | bytes 8388624 | tf_op jit(solution)/shard_map/all_gather | solution.py:22
  270.8 0.0 reduce-scatter.2.cloned.1.call-done
  270.8 0.0 copy-done.1
  270.8 0.0 copy-done.2
  270.8 10.5 %subtract_divide_fusion = f32[512,512]{0,1:T(8,128)S(1)} fusion(f32[512,512]{0,1:T(8,128)} %reduce-scatter.2.cloned.1.call-done, bf16[8192,512]{1,0:T(8,128)(2,1)} %all-gather.2.cloned.1.call-done, bf16[512,8192]{1,0:T(8,128)(2,1)} %param.8, s32[8192]{0:T(1024)S(1)} %reshape.12, s32[512]{0:T(512)S(1)} %dynamic_slice.6, f32[512]{0:T(512)S(1)} %copy-done.1, ...), kind=kOutput, calls=%fused_computation.12 | convolution fusion | flops 4304142336 | bytes 18913280 | tf_op jit(solution)/shard_map/dot_general | solution.py:21
  281.3 1.3 copy.11
Async XLA Ops:
  7.4 263.4 %all-gather.2.cloned.1.call-start = ((), (), s32[]{:S(2)}) async-start(), calls=%async_computation.1 | async-start | bytes 8912896 | tf_op jit(solution)/shard_map/all_gather | solution.py:22
  8.1 262.7 %reduce-scatter.2.cloned.1.call-start = ((), (), s32[]{:S(2)}) async-start(), calls=%async_computation.2 | async-start | bytes 17825792 | tf_op jit(solution)/shard_map/reduce_scatter | solution.py:28
  23.0 0.7 copy-start
  23.0 247.8 %copy-start.1 = (f32[512]{0:T(512)S(1)}, f32[512]{0:T(512)}, u32[]{:S(2)}) copy-start(f32[512]{0:T(512)} %param.12) | copy-start | bytes 6148
  23.0 247.8 %copy-start.2 = (f32[512]{0:T(512)S(1)}, f32[512]{0:T(512)}, u32[]{:S(2)}) copy-start(f32[512]{0:T(512)} %param.13) | copy-start | bytes 6148
Sparse Core Ops, SparseCore 0:
  10.9 259.8 all-gather.1
Sparse Core Ops, SparseCore 1:
  23.1 234.3 reduce-scatter.1
where the time goes:
time: 290 us
  waiting for transfers between devices  248 us (86%)
  matrix products  24.5 us (8%)
  between operations  14.9 us (5%)
  local copies, waits for them, and re-layouts  3.04 us (1%)
    all_gather x1, waiting for transfers between devices, per_device(): lax.all_gather(amplitudes, 'occ', axis=0, tiled=True)  247 us
    dot_general x1, matrix products, per_device(): lax.dot_general(slab_masked, amplitudes, contract_first, preferred_elemen...  14 us
    dot_general x1, matrix products, per_device(): lax.dot_general(lax.all_gather(amplitudes, 'occ', axis=0, tiled=True), ho...  10.5 us
  transfers between devices with their start and end apart: 2, of which 1 were waited for; matrix products, arithmetic and copies ran while one was open for 5% of the time, Pallas kernels for 0%

commit v1 on v0

v1 whole, which is shorter than its diff:
```python
import functools

import jax
import jax.numpy as jnp
from jax import lax
from jax.experimental import pallas as pl
from jax.experimental.pallas import tpu as pltpu
from jax.sharding import Mesh, PartitionSpec as P

TILE = 64
F32, BF16 = jnp.float32, jnp.bfloat16
AXES = ("zh", "y", "c", "zl", "x")
OCC, VIR = ("zh", "y", "c"), ("zl", "x")
NY, NC, NX, NZ = 4, 2, 4, 4
LIMIT = 48 * 1024 * 1024


def ring(n, d):
    return [(i, (i + d) % n) for i in range(n)]


def shift(a, axis, n, d):
    return lax.ppermute(a, axis, ring(n, d))


def params(n):
    return pltpu.CompilerParams(dimension_semantics=("arbitrary",) * n, vmem_limit_bytes=LIMIT)


def cost(blocks, n):
    return pl.CostEstimate(
        flops=2 * blocks * n**3, bytes_accessed=blocks * 2 * n * n * 2 + 4 * n * n, transcendentals=0
    )


def hole_kernel(idx, occ, klab0, klab1, w0, w1, t0, t1, *rest, has_acc):
    if has_acc:
        acc, out, masked = rest
    else:
        out, masked = rest
    j = pl.program_id(0)

    @pl.when(j == 0)
    def _():
        out[...] = acc[...] if has_acc else jnp.zeros_like(out)

    n = out.shape[0]
    for w, klab, t in ((w0, klab0, t0), (w1, klab1, t1)):
        for i in range(n // TILE):
            keep = (klab[...] == occ[idx[8] * (n // TILE) + i]).astype(F32).astype(BF16)
            rows = pl.ds(i * TILE, TILE)
            masked[rows, :] = w[rows, :] * keep
        out[...] += jnp.dot(masked[...], t[0], preferred_element_type=F32)


def hole_part(idx, occ, klab, w, own, other, acc=None):
    n = own.shape[1]
    in_specs = [
        pl.BlockSpec((1, n), lambda j, idx, occ: (0, idx[j])),
        pl.BlockSpec((1, n), lambda j, idx, occ: (0, idx[4 + j])),
        pl.BlockSpec((n, n), lambda j, idx, occ: (0, idx[j])),
        pl.BlockSpec((n, n), lambda j, idx, occ: (0, idx[4 + j])),
        pl.BlockSpec((1, n, n), lambda j, idx, occ: (j, 0, 0)),
        pl.BlockSpec((1, n, n), lambda j, idx, occ: (j, 0, 0)),
    ]
    args = [klab, klab, w, w, own, other]
    if acc is not None:
        in_specs.append(pl.BlockSpec((n, n), lambda j, idx, occ: (0, 0)))
        args.append(acc)
    return pl.pallas_call(
        functools.partial(hole_kernel, has_acc=acc is not None),
        out_shape=jax.ShapeDtypeStruct((n, n), F32),
        grid_spec=pltpu.PrefetchScalarGridSpec(
            num_scalar_prefetch=2,
            grid=(NY,),
            in_specs=in_specs,
            out_specs=pl.BlockSpec((n, n), lambda j, idx, occ: (0, 0)),
            scratch_shapes=[pltpu.VMEM((n, n), BF16)],
        ),
        compiler_params=params(1),
        cost_estimate=cost(2 * NY, n),
        name="hole_part",
    )(idx, occ, *args)


def particle_kernel(idx, vir, qlab, ta, va, vb, acc, *rest, last):
    if last:
        oe, ve, res, masked, out = rest
    else:
        out, masked = rest
    j = pl.program_id(0)

    @pl.when(j == 0)
    def _():
        out[...] = acc[...]

    n = out.shape[0]
    block = idx[j]
    for v, base in ((va, 4), (vb, 8)):
        for i in range(NY):
            s = idx[base + i]
            keep = (qlab[...] == vir[block * (n // TILE) + s]).astype(F32).astype(BF16)
            masked[pl.ds(pl.multiple_of(s * TILE, TILE), TILE), :] = v[i, 0] * keep
    out[...] += jnp.dot(ta[0], masked[...], preferred_element_type=F32)
    if last:

        @pl.when(j == pl.num_programs(0) - 1)
        def _():
            res[...] = out[...].T / (ve[...] - oe[...])


def particle_part(idx, vir, qlab, ta, va, vb, acc, energies=None):
    n = acc.shape[0]
    last = energies is not None
    full = lambda *shape: pl.BlockSpec(shape, lambda j, idx, vir: (0,) * len(shape))
    in_specs = [
        full(1, n),
        pl.BlockSpec((1, n, n), lambda j, idx, vir: (j, 0, 0)),
        pl.BlockSpec((NY, 1, TILE, n), lambda j, idx, vir: (0, idx[j], 0, 0)),
        pl.BlockSpec((NY, 1, TILE, n), lambda j, idx, vir: (0, idx[j], 0, 0)),
        full(n, n),
    ]
    args = [qlab, ta, va, vb, acc]
    scratch = [pltpu.VMEM((n, n), BF16)]
    if last:
        in_specs += [full(1, n), full(n, 1)]
        args += list(energies)
        scratch.append(pltpu.VMEM((n, n), F32))
    return pl.pallas_call(
        functools.partial(particle_kernel, last=last),
        out_shape=jax.ShapeDtypeStruct((n, n), F32),
        grid_spec=pltpu.PrefetchScalarGridSpec(
            num_scalar_prefetch=2,
            grid=(ta.shape[0],),
            in_specs=in_specs,
            out_specs=full(n, n),
            scratch_shapes=scratch,
        ),
        compiler_params=params(1),
        cost_estimate=cost(ta.shape[0], n),
        name="particle_last" if last else "particle_part",
    )(idx, vir, *args)


def y_gather(a):
    half = a.shape[0] // 2
    up, down = shift(a, "y", NY, 1), shift(a, "y", NY, -1)
    far_a, far_b = shift(up[:half], "y", NY, 1), shift(down[half:], "y", NY, -1)
    return jnp.stack([a, up, down, jnp.concatenate([far_a, far_b])])


def per_device(t, w, v, occ, vir, occ_energy, vir_energy):
    n = t.shape[0]
    zh, y, c, zl, x = (lax.axis_index(a).astype(jnp.int32) for a in AXES)
    z = ("zh", "zl")
    tiles = n // TILE
    v_rows = lax.dynamic_slice_in_dim(v, (y * NC + c) * TILE, TILE)
    v_own = lax.all_to_all(v_rows, VIR, 1, 0, tiled=True).reshape(NZ * NX, TILE, n)

    ta0 = lax.all_gather(t, "x")
    l1, r1 = shift(t, z, 8, 1), shift(t, z, 8, -1)
    own_y = y_gather(t)
    ta1 = lax.all_gather(jnp.where(zl == 0, r1, l1), "x")
    l2, r2 = shift(l1, z, 8, 1), shift(r1, z, 8, -1)
    ta2 = lax.all_gather(jnp.where(zl == 0, r2, jnp.where(zl == 3, l2, r1)), "x")
    l3, r3 = shift(l2, z, 8, 1), shift(r2, z, 8, -1)
    ta3 = lax.all_gather(jnp.where(zl == 0, r3, jnp.where(zl == 1, r2, jnp.where(zl == 2, l2, l3))), "x")
    half = n // 2
    far = jnp.concatenate([shift(l3[:half], z, 8, 1), shift(r3[half:], z, 8, -1)])

    own_c = shift(own_y, "c", NC, 1)
    va = y_gather(v_own)
    vb = shift(va, "c", NC, 1)
    far_y = y_gather(far)
    far_c = shift(far_y, "c", NC, 1)

    rel = jnp.array([0, 3, 1, 2], jnp.int32)
    ys = (y + rel) % NY
    o = (zh * NY + y) * NC + c
    i_own = (zh * NY + ys) * NC
    i_far = ((1 - zh) * NY + ys) * NC
    klab = jnp.repeat(occ, TILE)[None, :]
    acc = hole_part(jnp.concatenate([i_own + c, i_own + 1 - c, o[None]]), occ, klab, w, own_y, own_c)

    qlab = jnp.repeat(lax.dynamic_slice_in_dim(vir, (zl * NX + x) * tiles, tiles), TILE)[None, :]
    s_own, s_other = ys * NC + c, ys * NC + 1 - c
    xs = jnp.arange(NX, dtype=jnp.int32)
    src = [zl, jnp.where(zl == 0, 1, zl - 1), jnp.where(zl == 0, 2, jnp.where(zl == 3, 1, zl + 1)), jnp.where(zl <= 1, 3, 0)]
    ids = [jnp.concatenate([s * NX + xs, s_own, s_other]) for s in src]
    acc = hole_part(jnp.concatenate([i_far + c, i_far + 1 - c, o[None]]), occ, klab, w, far_y, far_c, acc)
    acc = particle_part(ids[0], vir, qlab, ta0, va, vb, acc)
    acc = particle_part(ids[1], vir, qlab, ta1, va, vb, acc)
    acc = particle_part(ids[2], vir, qlab, ta2, va, vb, acc)
    return particle_part(ids[3], vir, qlab, ta3, va, vb, acc, (occ_energy[None, :], vir_energy[:, None]))


def solution(mesh):
    fine = Mesh(mesh.devices.reshape(2, NY, NC, NZ, NX), AXES)
    placed = (P(OCC, VIR), P(OCC, None), P(VIR, None), P(), P(), P(OCC), P(VIR))
    return jax.shard_map(
        per_device, mesh=fine, in_specs=placed, out_specs=P(VIR, OCC), check_vma=False
    )
```

time: 290 us -> 213 us (0.73)
  the two profiles are of different devices: /device:TPU:65 before, /device:TPU:1 now
where the time goes in v1:
time: 213 us
  waiting for transfers between devices  81.7 us (38%)
  starting transfers between devices  40.3 us (19%)
  blocking collectives  30.5 us (14%)
  Pallas kernels  30.4 us (14%)
  between operations  13.6 us (6%)
  local copies, waits for them, and re-layouts  9.4 us (4%)
  other arithmetic  7.01 us (3%)
    ppermute x23, waiting for transfers between devices, shift(): return lax.ppermute(a, axis, ring(n, d))  80.8 us
    ppermute x23, starting transfers between devices, shift(): return lax.ppermute(a, axis, ring(n, d))  40.1 us
    all_to_all x1, blocking collectives, per_device(): lax.all_to_all(v_rows, VIR, 1, 0, tiled=True).reshape(NZ * NX, TILE, n)  30.5 us
    pallas_call x4, Pallas kernels, particle_part(): pl.pallas_call(functools.partial(particle_kernel, last=last), out_shape=j...  18.6 us
    pallas_call x2, Pallas kernels, hole_part(): pl.pallas_call(functools.partial(hole_kernel, has_acc=acc is not None), o...  11.8 us
    unnamed x35, local copies, waits for them, and re-layouts  6.55 us
    another operation x6, other arithmetic, y_gather(): return jnp.stack([a, up, down, jnp.concatenate([far_a, far_b])])  5.35 us
  transfers between devices with their start and end apart: 27, of which 12 were waited for; matrix products, arithmetic and copies ran while one was open for 5% of the time, Pallas kernels for 12%

profile of v1, /device:TPU:1, one launch (start us, length us, event | category | flops | bytes accessed | tf_op | source)
XLA Modules:
  0.0 212.8 jit_solution(17583386451291250757)
XLA Ops:
  9.8 4.0 %collective-permute-start = (bf16[512,512]{1,0:T(8,128)(2,1)}, bf16[512,512]{1,0:T(8,128)(2,1)S(1)}, u32[]{:S(2)}, u32[]{:S(2)}) collective-permute-start(bf16[512,512]{1,0:T(8,128)(2,1)} %param.8), channel_id=1, source_target_pairs={{0,140},{4,0},{8,4},{12,8},{128,12},{132,128},{136,132},{140,136},... | collective-permute-start | bytes 1572872 | tf_op jit(solution)/shard_map/ppermute | solution.py:23
  13.9 11.8 %collective-permute-done.3 = bf16[512,512]{1,0:T(8,128)(2,1)S(1)} collective-permute-done((bf16[512,512]{1,0:T(8,128)(2,1)}, bf16[512,512]{1,0:T(8,128)(2,1)S(1)}, u32[]{:S(2)}, u32[]{:S(2)}) %collective-permute-start.3) | collective-permute-done | bytes 524320 | tf_op jit(solution)/shard_map/ppermute | solution.py:23
  25.7 2.7 %collective-permute-start.1 = (bf16[512,512]{1,0:T(8,128)(2,1)S(1)}, bf16[512,512]{1,0:T(8,128)(2,1)S(1)}, u32[]{:S(2)}, u32[]{:S(2)}) collective-permute-start(bf16[512,512]{1,0:T(8,128)(2,1)S(1)} %collective-permute-done), channel_id=1, source_target_pairs={{0,140},{4,0},{8,4},{12,8},{128,12},{132,128},{136,132},{140,136},... | collective-permute-start | bytes 1572872 | tf_op jit(solution)/shard_map/ppermute | solution.py:23
  28.3 10.8 %collective-permute-done.4 = bf16[512,512]{1,0:T(8,128)(2,1)S(1)} collective-permute-done((bf16[512,512]{1,0:T(8,128)(2,1)S(1)}, bf16[512,512]{1,0:T(8,128)(2,1)S(1)}, u32[]{:S(2)}, u32[]{:S(2)}) %collective-permute-start.4) | collective-permute-done | bytes 524320 | tf_op jit(solution)/shard_map/ppermute | solution.py:23
  39.2 2.7 %collective-permute-start.2 = (bf16[512,512]{1,0:T(8,128)(2,1)S(1)}, bf16[512,512]{1,0:T(8,128)(2,1)S(1)}, u32[]{:S(2)}, u32[]{:S(2)}) collective-permute-start(bf16[512,512]{1,0:T(8,128)(2,1)S(1)} %collective-permute-done.1), channel_id=1, source_target_pairs={{0,140},{4,0},{8,4},{12,8},{128,12},{132,128},{136,132},{140,136},... | collective-permute-start | bytes 1572872 | tf_op jit(solution)/shard_map/ppermute | solution.py:23
  41.8 9.9 %collective-permute-done.5 = bf16[512,512]{1,0:T(8,128)(2,1)S(1)} collective-permute-done((bf16[512,512]{1,0:T(8,128)(2,1)S(1)}, bf16[512,512]{1,0:T(8,128)(2,1)S(1)}, u32[]{:S(2)}, u32[]{:S(2)}) %collective-permute-start.5) | collective-permute-done | bytes 524320 | tf_op jit(solution)/shard_map/ppermute | solution.py:23
  54.7 30.5 %all_to_all.16 = bf16[64,16,512]{2,0,1:T(8,128)(2,1)S(1)} all-to-all(bf16[64,16,512]{2,0,1:T(8,128)(2,1)S(1)} %bitcast.34), channel_id=1, replica_groups=mesh['zh'=2,'y'=4,'c'=2,'zl'=4,'x'=4] {'zl','x'}, dimensions={1} | all-to-all | bytes 2097152 | tf_op jit(solution)/shard_map/all_to_all | solution.py:158
  88.0 19.5 %collective-permute-done.6 = bf16[16,64,512]{2,1,0:T(8,128)(2,1)S(1)} collective-permute-done((bf16[16,64,512]{2,1,0:T(8,128)(2,1)S(1)}, bf16[16,64,512]{2,1,0:T(8,128)(2,1)S(1)}, u32[]{:S(2)}, u32[]{:S(2)}) %collective-permute-start.6) | collective-permute-done | bytes 1048608 | tf_op jit(solution)/shard_map/ppermute | solution.py:23
  107.7 2.7 %collective-permute-start.9 = (bf16[8,64,512]{2,1,0:T(8,128)(2,1)S(1)}, bf16[8,64,512]{2,1,0:T(8,128)(2,1)S(1)}, u32[]{:S(2)}, u32[]{:S(2)}) collective-permute-start(bf16[8,64,512]{2,1,0:T(8,128)(2,1)S(1)} %slice.33), channel_id=1, source_target_pairs={{0,96},{32,0},{64,32},{96,64},{1,97},{33,1},{65,33},{97,65},{2,98}... | collective-permute-start | bytes 1572872 | tf_op jit(solution)/shard_map/ppermute | solution.py:23
  110.4 7.6 %collective-permute-done.8 = bf16[8,64,512]{2,1,0:T(8,128)(2,1)S(1)} collective-permute-done((bf16[8,64,512]{2,1,0:T(8,128)(2,1)S(1)}, bf16[8,64,512]{2,1,0:T(8,128)(2,1)S(1)}, u32[]{:S(2)}, u32[]{:S(2)}) %collective-permute-start.8) | collective-permute-done | bytes 524320 | tf_op jit(solution)/shard_map/ppermute | solution.py:23
  120.4 5.3 %collective-permute-start.10 = (bf16[4,16,64,512]{3,2,1,0:T(8,128)(2,1)}, bf16[4,16,64,512]{3,2,1,0:T(8,128)(2,1)}, u32[]{:S(2)}, u32[]{:S(2)}) collective-permute-start(bf16[4,16,64,512]{3,2,1,0:T(8,128)(2,1)} %pad_maximum_fusion.va), channel_id=1, source_target_pairs={{0,16},{16,0},{1,17},{17,1},{2,18},{18,2},{3,19},{19,3},{4,20},{20... | collective-permute-start | bytes 12582920 | tf_op jit(solution)/shard_map/ppermute | solution.py:23
  131.8 3.8 %collective-permute-done.11 = bf16[256,512]{1,0:T(8,128)(2,1)S(1)} collective-permute-done((bf16[256,512]{1,0:T(8,128)(2,1)S(1)}, bf16[256,512]{1,0:T(8,128)(2,1)S(1)}, u32[]{:S(2)}, u32[]{:S(2)}) %collective-permute-start.11) | collective-permute-done | bytes 262176 | tf_op jit(solution)/shard_map/ppermute | solution.py:23
  137.3 2.7 %collective-permute-start.14 = (bf16[512,512]{1,0:T(8,128)(2,1)S(1)}, bf16[512,512]{1,0:T(8,128)(2,1)S(1)}, u32[]{:S(2)}, u32[]{:S(2)}) collective-permute-start(bf16[512,512]{1,0:T(8,128)(2,1)S(1)} %constant_dynamic-update-slice_fusion), channel_id=1, source_target_pairs={{0,96},{32,0},{64,32},{96,64},{1,97},{33,1},{65,33},{97,65},{2,98}... | collective-permute-start | bytes 1572872 | tf_op jit(solution)/shard_map/ppermute | solution.py:23
  140.0 3.7 %collective-permute-done.18 = bf16[512,512]{1,0:T(8,128)(2,1)S(1)} collective-permute-done((bf16[512,512]{1,0:T(8,128)(2,1)S(1)}, bf16[512,512]{1,0:T(8,128)(2,1)S(1)}, u32[]{:S(2)}, u32[]{:S(2)}) %collective-permute-start.18) | collective-permute-done | bytes 524320 | tf_op jit(solution)/shard_map/ppermute | solution.py:23
  144.5 2.7 %collective-permute-start.21 = (bf16[256,512]{1,0:T(8,128)(2,1)}, bf16[256,512]{1,0:T(8,128)(2,1)}, u32[]{:S(2)}, u32[]{:S(2)}) collective-permute-start(bf16[256,512]{1,0:T(8,128)(2,1)} %slice.39), channel_id=1, source_target_pairs={{0,96},{32,0},{64,32},{96,64},{1,97},{33,1},{65,33},{97,65},{2,98}... | collective-permute-start | bytes 786440 | tf_op jit(solution)/shard_map/ppermute | solution.py:23
  147.2 7.7 %collective-permute-done.13 = bf16[512,512]{1,0:T(8,128)(2,1)S(1)} collective-permute-done((bf16[512,512]{1,0:T(8,128)(2,1)S(1)}, bf16[512,512]{1,0:T(8,128)(2,1)S(1)}, u32[]{:S(2)}, u32[]{:S(2)}) %collective-permute-start.13) | collective-permute-done | bytes 524320 | tf_op jit(solution)/shard_map/ppermute | solution.py:23
  155.1 2.7 %collective-permute-start.16 = (bf16[256,512]{1,0:T(8,128)(2,1)S(1)}, bf16[256,512]{1,0:T(8,128)(2,1)S(1)}, u32[]{:S(2)}, u32[]{:S(2)}) collective-permute-start(bf16[256,512]{1,0:T(8,128)(2,1)S(1)} %slice.37), channel_id=1, source_target_pairs={{0,96},{32,0},{64,32},{96,64},{1,97},{33,1},{65,33},{97,65},{2,98}... | collective-permute-start | bytes 786440 | tf_op jit(solution)/shard_map/ppermute | solution.py:23
  157.8 2.8 %collective-permute-done.20 = bf16[256,512]{1,0:T(8,128)(2,1)} collective-permute-done((bf16[256,512]{1,0:T(8,128)(2,1)S(1)}, bf16[256,512]{1,0:T(8,128)(2,1)}, u32[]{:S(2)}, u32[]{:S(2)}) %collective-permute-start.20) | collective-permute-done | bytes 262176 | tf_op jit(solution)/shard_map/ppermute | solution.py:23
  169.3 6.1 %hole_part.2.rest_0_ = f32[512,512]{1,0:T(8,128)S(1)} custom-call(s32[9]{0:T(128)S(1)} %add_add_fusion.5.idx, s32[128]{0:T(128)S(1)} %copy-done.5, s32[1,8192]{1,0:T(1,128)S(1)} %broadcast_in_dim_reshape.7.klab0.klab1, s32[1,8192]{1,0:T(1,128)S(1)} %broadcast_in_dim_reshape.7.klab0.klab1, bf16[512,8192]{1,0:T(8,128)(2,1)} %w1.3, bf16[512,8192]{1,0:T(8,128)(2,1)} %w1.3, ...), custom_call_target="tpu_custom_call" | custom-call | flops 2147483648 | bytes 9437184 | tf_op jit(solution)/shard_map/hole_part/pallas_call | solution.py:70
  175.5 5.7 %hole_part.3.acc = f32[512,512]{1,0:T(8,128)S(1)} custom-call(s32[9]{0:T(128)S(1)} %add_add_fusion.4.idx, s32[128]{0:T(128)S(1)} %copy-done.5, s32[1,8192]{1,0:T(1,128)S(1)} %broadcast_in_dim_reshape.7.klab0.klab1, s32[1,8192]{1,0:T(1,128)S(1)} %broadcast_in_dim_reshape.7.klab0.klab1, bf16[512,8192]{1,0:T(8,128)(2,1)} %w1.3, bf16[512,8192]{1,0:T(8,128)(2,1)} %w1.3, ...), custom_call_target="tpu_custom_call" | custom-call | flops 2147483648 | bytes 9437184 | tf_op jit(solution)/shard_map/hole_part/pallas_call | solution.py:70
  182.8 4.3 %particle_part.3.acc = f32[512,512]{1,0:T(8,128)S(1)} custom-call(s32[12]{0:T(128)S(1)} %get-tuple-element.10.idx, s32[128]{0:T(128)S(1)} %copy-done.4, s32[1,512]{1,0:T(1,128)S(1)} %broadcast_in_dim_reshape.6.qlab, bf16[4,512,512]{2,1,0:T(8,128)(2,1)S(1)} %bitcast.28, bf16[4,16,64,512]{3,2,1,0:T(8,128)(2,1)} %pad_maximum_fusion.va, ...), custom_call_target="tpu_custom_call" | custom-call | flops 1073741824 | bytes 5242880 | tf_op jit(solution)/shard_map/particle_part/pallas_call | solution.py:129
  188.7 4.3 %particle_part.4.acc = f32[512,512]{1,0:T(8,128)S(1)} custom-call(s32[12]{0:T(128)S(1)} %get-tuple-element.12.idx, s32[128]{0:T(128)S(1)} %copy-done.4, s32[1,512]{1,0:T(1,128)S(1)} %broadcast_in_dim_reshape.6.qlab, bf16[4,512,512]{2,1,0:T(8,128)(2,1)S(1)} %bitcast.29, bf16[4,16,64,512]{3,2,1,0:T(8,128)(2,1)} %pad_maximum_fusion.va, ...), custom_call_target="tpu_custom_call" | custom-call | flops 1073741824 | bytes 5242880 | tf_op jit(solution)/shard_map/particle_part/pallas_call | solution.py:129
  194.6 4.3 %particle_part.5.acc = f32[512,512]{1,0:T(8,128)S(1)} custom-call(s32[12]{0:T(128)S(1)} %get-tuple-element.11.idx, s32[128]{0:T(128)S(1)} %copy-done.4, s32[1,512]{1,0:T(1,128)S(1)} %broadcast_in_dim_reshape.6.qlab, bf16[4,512,512]{2,1,0:T(8,128)(2,1)S(1)} %bitcast.30, bf16[4,16,64,512]{3,2,1,0:T(8,128)(2,1)} %pad_maximum_fusion.va, ...), custom_call_target="tpu_custom_call" | custom-call | flops 1073741824 | bytes 5242880 | tf_op jit(solution)/shard_map/particle_part/pallas_call | solution.py:129
  200.6 5.7 %particle_last.1 = f32[512,512]{1,0:T(8,128)} custom-call(s32[12]{0:T(128)S(1)} %add_add_fusion.idx, s32[128]{0:T(128)S(1)} %copy-done.4, s32[1,512]{1,0:T(1,128)S(1)} %broadcast_in_dim_reshape.6.qlab, bf16[4,512,512]{2,1,0:T(8,128)(2,1)S(1)} %bitcast.31, bf16[4,16,64,512]{3,2,1,0:T(8,128)(2,1)} %pad_maximum_fusion.va, ...), custom_call_target="tpu_custom_call" | custom-call | flops 1073741824 | bytes 5242880 | tf_op jit(solution)/shard_map/particle_last/pallas_call | solution.py:129
  (109 shorter events, 35.2 us)
Async XLA Ops:
  6.5 174.7 %all-gather.15.cloned.1.call-start = ((), (), s32[]{:S(2)}) async-start(), calls=%async_computation.4 | async-start | bytes 2621440 | tf_op jit(solution)/shard_map/all_gather | solution.py:160
  7.3 179.9 %all-gather.13.cloned.1.call-start = ((), (), s32[]{:S(2)}) async-start(), calls=%async_computation.3 | async-start | bytes 2621440 | tf_op jit(solution)/shard_map/all_gather | solution.py:163
  7.3 18.3 %collective-permute-start.3 = (bf16[512,512]{1,0:T(8,128)(2,1)}, bf16[512,512]{1,0:T(8,128)(2,1)S(1)}, u32[]{:S(2)}, u32[]{:S(2)}) collective-permute-start(bf16[512,512]{1,0:T(8,128)(2,1)} %param.8), channel_id=1, source_target_pairs={{0,4},{4,8},{8,12},{12,128},{128,132},{132,136},{136,140},{140,0},... | collective-permute-start | bytes 1572872 | tf_op jit(solution)/shard_map/ppermute | solution.py:23
  9.8 15.8 %collective-permute-start = (bf16[512,512]{1,0:T(8,128)(2,1)}, bf16[512,512]{1,0:T(8,128)(2,1)S(1)}, u32[]{:S(2)}, u32[]{:S(2)}) collective-permute-start(bf16[512,512]{1,0:T(8,128)(2,1)} %param.8), channel_id=1, source_target_pairs={{0,140},{4,0},{8,4},{12,8},{128,12},{132,128},{136,132},{140,136},... | collective-permute-start | bytes 1572872 | tf_op jit(solution)/shard_map/ppermute | solution.py:23
  25.6 13.5 %collective-permute-start.4 = (bf16[512,512]{1,0:T(8,128)(2,1)S(1)}, bf16[512,512]{1,0:T(8,128)(2,1)S(1)}, u32[]{:S(2)}, u32[]{:S(2)}) collective-permute-start(bf16[512,512]{1,0:T(8,128)(2,1)S(1)} %collective-permute-done.3), channel_id=1, source_target_pairs={{0,4},{4,8},{8,12},{12,128},{128,132},{132,136},{136,140},{140,0},... | collective-permute-start | bytes 1572872 | tf_op jit(solution)/shard_map/ppermute | solution.py:23
  25.7 13.5 %collective-permute-start.1 = (bf16[512,512]{1,0:T(8,128)(2,1)S(1)}, bf16[512,512]{1,0:T(8,128)(2,1)S(1)}, u32[]{:S(2)}, u32[]{:S(2)}) collective-permute-start(bf16[512,512]{1,0:T(8,128)(2,1)S(1)} %collective-permute-done), channel_id=1, source_target_pairs={{0,140},{4,0},{8,4},{12,8},{128,12},{132,128},{136,132},{140,136},... | collective-permute-start | bytes 1572872 | tf_op jit(solution)/shard_map/ppermute | solution.py:23
  39.2 12.6 %collective-permute-start.5 = (bf16[512,512]{1,0:T(8,128)(2,1)S(1)}, bf16[512,512]{1,0:T(8,128)(2,1)S(1)}, u32[]{:S(2)}, u32[]{:S(2)}) collective-permute-start(bf16[512,512]{1,0:T(8,128)(2,1)S(1)} %collective-permute-done.4), channel_id=1, source_target_pairs={{0,4},{4,8},{8,12},{12,128},{128,132},{132,136},{136,140},{140,0},... | collective-permute-start | bytes 1572872 | tf_op jit(solution)/shard_map/ppermute | solution.py:23
  39.2 12.6 %collective-permute-start.2 = (bf16[512,512]{1,0:T(8,128)(2,1)S(1)}, bf16[512,512]{1,0:T(8,128)(2,1)S(1)}, u32[]{:S(2)}, u32[]{:S(2)}) collective-permute-start(bf16[512,512]{1,0:T(8,128)(2,1)S(1)} %collective-permute-done.1), channel_id=1, source_target_pairs={{0,140},{4,0},{8,4},{12,8},{128,12},{132,128},{136,132},{140,136},... | collective-permute-start | bytes 1572872 | tf_op jit(solution)/shard_map/ppermute | solution.py:23
  53.2 139.8 %all-gather.11.cloned.1.call-start = ((), (), s32[]{:S(2)}) async-start(), calls=%async_computation.2 | async-start | bytes 2621440 | tf_op jit(solution)/shard_map/all_gather | solution.py:165
  85.2 22.3 %collective-permute-start.6 = (bf16[16,64,512]{2,1,0:T(8,128)(2,1)S(1)}, bf16[16,64,512]{2,1,0:T(8,128)(2,1)S(1)}, u32[]{:S(2)}, u32[]{:S(2)}) collective-permute-start(bf16[16,64,512]{2,1,0:T(8,128)(2,1)S(1)} %bitcast.35), channel_id=1, source_target_pairs={{0,32},{32,64},{64,96},{96,0},{1,33},{33,65},{65,97},{97,1},{2,34}... | collective-permute-start | bytes 3145736 | tf_op jit(solution)/shard_map/ppermute | solution.py:23
  86.5 21.2 %collective-permute-start.7 = (bf16[16,64,512]{2,1,0:T(8,128)(2,1)S(1)}, bf16[16,64,512]{2,1,0:T(8,128)(2,1)S(1)}, u32[]{:S(2)}, u32[]{:S(2)}) collective-permute-start(bf16[16,64,512]{2,1,0:T(8,128)(2,1)S(1)} %bitcast.36), channel_id=1, source_target_pairs={{0,96},{32,0},{64,32},{96,64},{1,97},{33,1},{65,33},{97,65},{2,98}... | collective-permute-start | bytes 3145736 | tf_op jit(solution)/shard_map/ppermute | solution.py:23
  87.9 111.0 %all-gather.9.cloned.1.call-start = ((), (), s32[]{:S(2)}) async-start(), calls=%async_computation.1 | async-start | bytes 2621440 | tf_op jit(solution)/shard_map/all_gather | solution.py:167
  107.6 10.4 %collective-permute-start.8 = (bf16[8,64,512]{2,1,0:T(8,128)(2,1)S(1)}, bf16[8,64,512]{2,1,0:T(8,128)(2,1)S(1)}, u32[]{:S(2)}, u32[]{:S(2)}) collective-permute-start(bf16[8,64,512]{2,1,0:T(8,128)(2,1)S(1)} %slice.32), channel_id=1, source_target_pairs={{0,32},{32,64},{64,96},{96,0},{1,33},{33,65},{65,97},{97,1},{2,34}... | collective-permute-start | bytes 1572872 | tf_op jit(solution)/shard_map/ppermute | solution.py:23
  107.7 10.3 %collective-permute-start.9 = (bf16[8,64,512]{2,1,0:T(8,128)(2,1)S(1)}, bf16[8,64,512]{2,1,0:T(8,128)(2,1)S(1)}, u32[]{:S(2)}, u32[]{:S(2)}) collective-permute-start(bf16[8,64,512]{2,1,0:T(8,128)(2,1)S(1)} %slice.33), channel_id=1, source_target_pairs={{0,96},{32,0},{64,32},{96,64},{1,97},{33,1},{65,33},{97,65},{2,98}... | collective-permute-start | bytes 1572872 | tf_op jit(solution)/shard_map/ppermute | solution.py:23
  120.4 60.8 %collective-permute-start.10 = (bf16[4,16,64,512]{3,2,1,0:T(8,128)(2,1)}, bf16[4,16,64,512]{3,2,1,0:T(8,128)(2,1)}, u32[]{:S(2)}, u32[]{:S(2)}) collective-permute-start(bf16[4,16,64,512]{3,2,1,0:T(8,128)(2,1)} %pad_maximum_fusion.va), channel_id=1, source_target_pairs={{0,16},{16,0},{1,17},{17,1},{2,18},{18,2},{3,19},{19,3},{4,20},{20... | collective-permute-start | bytes 12582920 | tf_op jit(solution)/shard_map/ppermute | solution.py:23
  125.7 9.8 %collective-permute-start.11 = (bf16[256,512]{1,0:T(8,128)(2,1)S(1)}, bf16[256,512]{1,0:T(8,128)(2,1)S(1)}, u32[]{:S(2)}, u32[]{:S(2)}) collective-permute-start(bf16[256,512]{1,0:T(8,128)(2,1)S(1)} %slice.34), channel_id=1, source_target_pairs={{0,4},{4,8},{8,12},{12,128},{128,132},{132,136},{136,140},{140,0},... | collective-permute-start | bytes 786440 | tf_op jit(solution)/shard_map/ppermute | solution.py:23
  129.0 14.7 %collective-permute-start.18 = (bf16[512,512]{1,0:T(8,128)(2,1)S(1)}, bf16[512,512]{1,0:T(8,128)(2,1)S(1)}, u32[]{:S(2)}, u32[]{:S(2)}) collective-permute-start(bf16[512,512]{1,0:T(8,128)(2,1)S(1)} %copy-done.7), channel_id=1, source_target_pairs={{0,32},{32,64},{64,96},{96,0},{1,33},{33,65},{65,97},{97,1},{2,34}... | collective-permute-start | bytes 1572872 | tf_op jit(solution)/shard_map/ppermute | solution.py:23
  129.9 13.9 %collective-permute-start.19 = (bf16[512,512]{1,0:T(8,128)(2,1)S(1)}, bf16[512,512]{1,0:T(8,128)(2,1)S(1)}, u32[]{:S(2)}, u32[]{:S(2)}) collective-permute-start(bf16[512,512]{1,0:T(8,128)(2,1)S(1)} %copy-done.7), channel_id=1, source_target_pairs={{0,96},{32,0},{64,32},{96,64},{1,97},{33,1},{65,33},{97,65},{2,98}... | collective-permute-start | bytes 1572872 | tf_op jit(solution)/shard_map/ppermute | solution.py:23
  137.0 17.9 %collective-permute-start.13 = (bf16[512,512]{1,0:T(8,128)(2,1)S(1)}, bf16[512,512]{1,0:T(8,128)(2,1)S(1)}, u32[]{:S(2)}, u32[]{:S(2)}) collective-permute-start(bf16[512,512]{1,0:T(8,128)(2,1)S(1)} %constant_dynamic-update-slice_fusion), channel_id=1, source_target_pairs={{0,32},{32,64},{64,96},{96,0},{1,33},{33,65},{65,97},{97,1},{2,34}... | collective-permute-start | bytes 1572872 | tf_op jit(solution)/shard_map/ppermute | solution.py:23
  137.3 17.8 %collective-permute-start.14 = (bf16[512,512]{1,0:T(8,128)(2,1)S(1)}, bf16[512,512]{1,0:T(8,128)(2,1)S(1)}, u32[]{:S(2)}, u32[]{:S(2)}) collective-permute-start(bf16[512,512]{1,0:T(8,128)(2,1)S(1)} %constant_dynamic-update-slice_fusion), channel_id=1, source_target_pairs={{0,96},{32,0},{64,32},{96,64},{1,97},{33,1},{65,33},{97,65},{2,98}... | collective-permute-start | bytes 1572872 | tf_op jit(solution)/shard_map/ppermute | solution.py:23
  143.7 16.9 %collective-permute-start.20 = (bf16[256,512]{1,0:T(8,128)(2,1)S(1)}, bf16[256,512]{1,0:T(8,128)(2,1)}, u32[]{:S(2)}, u32[]{:S(2)}) collective-permute-start(bf16[256,512]{1,0:T(8,128)(2,1)S(1)} %slice.38), channel_id=1, source_target_pairs={{0,32},{32,64},{64,96},{96,0},{1,33},{33,65},{65,97},{97,1},{2,34}... | collective-permute-start | bytes 786440 | tf_op jit(solution)/shard_map/ppermute | solution.py:23
  144.5 16.1 %collective-permute-start.21 = (bf16[256,512]{1,0:T(8,128)(2,1)}, bf16[256,512]{1,0:T(8,128)(2,1)}, u32[]{:S(2)}, u32[]{:S(2)}) collective-permute-start(bf16[256,512]{1,0:T(8,128)(2,1)} %slice.39), channel_id=1, source_target_pairs={{0,96},{32,0},{64,32},{96,64},{1,97},{33,1},{65,33},{97,65},{2,98}... | collective-permute-start | bytes 786440 | tf_op jit(solution)/shard_map/ppermute | solution.py:23
  154.9 11.3 %collective-permute-start.15 = (bf16[256,512]{1,0:T(8,128)(2,1)S(1)}, bf16[256,512]{1,0:T(8,128)(2,1)S(1)}, u32[]{:S(2)}, u32[]{:S(2)}) collective-permute-start(bf16[256,512]{1,0:T(8,128)(2,1)S(1)} %slice.36), channel_id=1, source_target_pairs={{0,32},{32,64},{64,96},{96,0},{1,33},{33,65},{65,97},{97,1},{2,34}... | collective-permute-start | bytes 786440 | tf_op jit(solution)/shard_map/ppermute | solution.py:23
  155.1 11.2 %collective-permute-start.16 = (bf16[256,512]{1,0:T(8,128)(2,1)S(1)}, bf16[256,512]{1,0:T(8,128)(2,1)S(1)}, u32[]{:S(2)}, u32[]{:S(2)}) collective-permute-start(bf16[256,512]{1,0:T(8,128)(2,1)S(1)} %slice.37), channel_id=1, source_target_pairs={{0,96},{32,0},{64,32},{96,64},{1,97},{33,1},{65,33},{97,65},{2,98}... | collective-permute-start | bytes 786440 | tf_op jit(solution)/shard_map/ppermute | solution.py:23
  (20 other events, 126.4 us)
Sparse Core Ops, SparseCore 0:
  9.2 37.1 all-gather.14
  53.3 41.3 all-gather.12
  96.5 32.0 all-gather.10
  147.3 30.4 all-gather.8

commit v2 on v1

v2 whole, which is shorter than its diff:
```python
import functools

import jax
import jax.numpy as jnp
from jax import lax
from jax.experimental import pallas as pl
from jax.experimental.pallas import tpu as pltpu
from jax.sharding import Mesh, PartitionSpec as P

TILE = 64
F32, BF16 = jnp.float32, jnp.bfloat16
AXES = ("zh", "y", "c", "zl", "x")
OCC, VIR, YC = ("zh", "y", "c"), ("zl", "x"), ("y", "c")
NY, NC, NX, NZ = 4, 2, 4, 4
LIMIT = 60 * 1024 * 1024


def ring(n, d):
    return [(i, (i + d) % n) for i in range(n)]


def shift(a, axis, n, d):
    return lax.ppermute(a, axis, ring(n, d))


def params(n):
    return pltpu.CompilerParams(dimension_semantics=("arbitrary",) * n, vmem_limit_bytes=LIMIT)


def cost(blocks, n):
    return pl.CostEstimate(
        flops=2 * blocks * n**3, bytes_accessed=blocks * 2 * n * n * 2 + 4 * n * n, transcendentals=0
    )


def mask_of(labels, label):
    return (labels == label).astype(F32).astype(BF16)


def far_kernel(idx, occ, klab, w, t, acc, out, masked):
    j = pl.program_id(0)
    n = out.shape[0]
    for i in range(n // TILE):
        rows = pl.ds(i * TILE, TILE)
        masked[rows, :] = w[rows, :] * mask_of(klab[...], occ[idx[1] * (n // TILE) + i])
    part = jnp.dot(masked[...], t[...], preferred_element_type=F32)

    @pl.when(j == 0)
    def _():
        out[...] = acc[...] + part

    @pl.when(j > 0)
    def _():
        out[...] += part


def full(*shape):
    return pl.BlockSpec(shape, lambda *_: (0,) * len(shape))


def hole_kernel(idx, occ, klab, w, pair, g1, h1, g2, h2, *rest, has_acc):
    acc, (out, masked) = (rest[0], rest[1:]) if has_acc else (None, rest)
    j = pl.program_id(0)
    n = out.shape[0]
    core = idx[4]
    for i in range(n // TILE):
        rows = pl.ds(i * TILE, TILE)
        masked[rows, :] = w[rows, :] * mask_of(klab[...], occ[idx[5] * (n // TILE) + i])

    for step, t in enumerate((pair, g1, h1)):

        @pl.when(j == step)
        def _(step=step, t=t):
            part = jnp.dot(masked[...], t[...], preferred_element_type=F32)
            if step:
                out[...] += part
            elif has_acc:
                out[...] = acc[...] + part
            else:
                out[...] = part

    @pl.when(j == 3)
    def _():
        mine = masked[:, pl.ds(pl.multiple_of(core * n, n), n)]
        other = masked[:, pl.ds(pl.multiple_of((1 - core) * n, n), n)]
        out[...] += jnp.dot(mine, g2[...], preferred_element_type=F32) + jnp.dot(
            other, h2[...], preferred_element_type=F32
        )


def hole_part(idx, occ, klab, w, pair, g1, h1, g2, h2, acc=None):
    n = w.shape[0]
    in_specs = [
        pl.BlockSpec((1, 2 * n), lambda j, idx, occ: (0, idx[j])),
        pl.BlockSpec((n, 2 * n), lambda j, idx, occ: (0, idx[j])),
        full(2 * n, n),
        full(2 * n, n),
        full(2 * n, n),
        full(n, n),
        full(n, n),
    ]
    args = [klab, w, pair, g1, h1, g2, h2]
    if acc is not None:
        in_specs.append(full(n, n))
        args.append(acc)
    return pl.pallas_call(
        functools.partial(hole_kernel, has_acc=acc is not None),
        out_shape=jax.ShapeDtypeStruct((n, n), F32),
        grid_spec=pltpu.PrefetchScalarGridSpec(
            num_scalar_prefetch=2,
            grid=(NY,),
            in_specs=in_specs,
            out_specs=full(n, n),
            scratch_shapes=[pltpu.VMEM((n, 2 * n), BF16)],
        ),
        compiler_params=params(1),
        cost_estimate=cost(2 * NY, n),
        name="hole_part",
    )(idx, occ, *args)


def far_part(idx, occ, klab, w, t, acc):
    n = w.shape[0]
    steps = 2
    block = t.shape[0] // steps
    return pl.pallas_call(
        far_kernel,
        out_shape=jax.ShapeDtypeStruct((n, n), F32),
        grid_spec=pltpu.PrefetchScalarGridSpec(
            num_scalar_prefetch=2,
            grid=(steps,),
            in_specs=[
                pl.BlockSpec((1, block), lambda j, idx, occ: (0, idx[0] * steps + j)),
                pl.BlockSpec((n, block), lambda j, idx, occ: (0, idx[0] * steps + j)),
                pl.BlockSpec((block, n), lambda j, idx, occ: (j, 0)),
                full(n, n),
            ],
            out_specs=full(n, n),
            scratch_shapes=[pltpu.VMEM((n, block), BF16)],
        ),
        compiler_params=params(1),
        cost_estimate=cost(t.shape[0] // n, n),
        name="far_part",
    )(idx, occ, klab, w, t, acc)


def particle_kernel(idx, vir, qlab, *refs, count, split, last):
    nt = 2 if split else count
    tas, (pair, g1, h1, g2, h2, acc), rest = refs[:nt], refs[nt : nt + 6], refs[nt + 6 :]
    if last:
        oe, ve, out, masked, total = rest
    else:
        total, masked = rest
    j = pl.program_id(0)
    n = total.shape[0]
    tiles = n // TILE
    for k in range(count):
        label = lambda s: vir[(idx[j] * NX + idx[4 + k]) * tiles + s]
        b = 0 if count == 1 else idx[4 + k]
        for i, v in enumerate((pair, g1, h1)):
            s = idx[8 + i] * NC
            for e in range(NC):
                rows = pl.ds(pl.multiple_of(k * n + (s + e) * TILE, TILE), TILE)
                masked[rows, :] = v[e, b] * mask_of(qlab[...], label(s + e))
        for v, core in ((g2, idx[12]), (h2, 1 - idx[12])):
            s = idx[11] * NC + core
            rows = pl.ds(pl.multiple_of(k * n + s * TILE, TILE), TILE)
            masked[rows, :] = v[b] * mask_of(qlab[...], label(s))

    @pl.when(j == 0)
    def _():
        total[...] = acc[...]

    if split:
        for i, ta in enumerate(tas):
            rows = pl.ds(i * (n // 2), n // 2)
            total[rows, :] += jnp.dot(ta[0], masked[...], preferred_element_type=F32)
    else:
        blocks = jnp.concatenate([ta[0] for ta in tas], axis=1)
        total[...] += jnp.dot(blocks, masked[...], preferred_element_type=F32)

    if last:

        @pl.when(j == pl.num_programs(0) - 1)
        def _():
            out[...] = total[...].T / (ve[...] - oe[...])


def particle_part(idx, vir, qlab, tas, vs, acc, split=False, energies=None):
    n = acc.shape[0]
    last = energies is not None
    steps, count = tas[0].shape[0], 1 if split else len(tas)
    wide = pl.BlockSpec((NC, NX, TILE, n), lambda j, idx, vir: (0, idx[j], 0, 0))
    slim = pl.BlockSpec((NX, TILE, n), lambda j, idx, vir: (idx[j], 0, 0))
    if count == 1:
        wide = pl.BlockSpec((NC, 1, TILE, n), lambda j, idx, vir: (0, idx[j] * NX + idx[4], 0, 0))
        slim = pl.BlockSpec((1, TILE, n), lambda j, idx, vir: (idx[j] * NX + idx[4], 0, 0))
    at = pl.BlockSpec((1,) + tas[0].shape[1:], lambda j, *_: (j, 0, 0))
    in_specs = [full(1, n), *([at] * len(tas)), wide, wide, wide, slim, slim, full(n, n)]
    args = [qlab, *tas, *vs, acc]
    scratch = [pltpu.VMEM((count * n, n), BF16)]
    if last:
        in_specs += [full(1, n), full(n, 1)]
        args += list(energies)
        scratch.append(pltpu.VMEM((n, n), F32))
    return pl.pallas_call(
        functools.partial(particle_kernel, count=count, split=split, last=last),
        out_shape=jax.ShapeDtypeStruct((n, n), F32),
        grid_spec=pltpu.PrefetchScalarGridSpec(
            num_scalar_prefetch=2,
            grid=(steps,),
            in_specs=in_specs,
            out_specs=full(n, n),
            scratch_shapes=scratch,
        ),
        compiler_params=params(1),
        cost_estimate=cost(count * steps, n),
        name="particle_last" if last else "particle_part",
    )(idx, vir, *args)


def pick_kernel(idx, a, out):
    out[...] = a[...]


def pick(a, idx):
    block = (1,) + a.shape[1:]
    return pl.pallas_call(
        pick_kernel,
        out_shape=jax.ShapeDtypeStruct(idx.shape + a.shape[1:], a.dtype),
        grid_spec=pltpu.PrefetchScalarGridSpec(
            num_scalar_prefetch=1,
            grid=idx.shape,
            in_specs=[pl.BlockSpec(block, lambda j, idx: (idx[j], 0, 0))],
            out_specs=pl.BlockSpec(block, lambda j, idx: (j, 0, 0)),
        ),
        compiler_params=params(1),
        name="pick",
    )(idx, a)


AROUND = [(y * NC + c, (y + 1 - 2 * c) % NY * NC + c) for y in range(NY) for c in range(NC)]


def swap(a):
    return lax.ppermute(a, "c", ring(NC, 1))


def around(a):
    return lax.ppermute(a, YC, AROUND)


def tie(*arrays):
    return lax.optimization_barrier(arrays)


def per_device(t, w, v, occ, vir, occ_energy, vir_energy):
    n = t.shape[0]
    zh, y, c, zl, x = (lax.axis_index(a).astype(jnp.int32) for a in AXES)
    z = ("zh", "zl")
    tiles, half = n // TILE, n // 2
    both = lambda a, b: jnp.where(c == 0, jnp.stack([a, b]), jnp.stack([b, a]))
    mine = lambda a: jnp.where(c == 0, a[0], a[1])

    zag = lax.all_gather(t, z)
    v_rows = lax.dynamic_slice_in_dim(v, (y * NC + c) * TILE, TILE)
    v_own = lax.all_to_all(v_rows, VIR, 1, 0, tiled=True).reshape(NZ * NX, TILE, n)
    x1, x3 = shift(t, "x", NX, 1), shift(t, "x", NX, -1)
    pair = both(t, swap(t))
    g1 = around(pair)
    x1, x3, g1 = tie(x1, x3, g1)
    x2a, x2b = shift(x1[:half], "x", NX, 1), shift(x3[half:], "x", NX, -1)
    g2, h1 = around(mine(g1)), swap(g1)
    x2a, x2b, g2, h1, v_own = tie(x2a, x2b, g2, h1, v_own)

    o = (zh * NY + y) * NC + c
    klab = jnp.repeat(occ, TILE)[None, :]
    flat = lambda a: a.reshape(-1, n)
    near = y + 2 * c - 1
    ys = jnp.stack([y, near, 2 * y - near, y + 2]) % NY
    xs = (x + jnp.array([0, 3, 1, 2], jnp.int32)) % NX

    v_pair = both(v_own, swap(v_own))
    vg1 = around(v_pair)
    x2 = jnp.concatenate([x2a, x2b])
    h2 = swap(g2)
    i_own = jnp.concatenate([zh * NY + ys, c[None], o[None]])
    acc = hole_part(i_own, occ, klab, w, flat(pair), flat(g1), flat(h1), g2, h2)
    others = pick(zag, zh * NZ + (zl + 1 + jnp.arange(NZ - 1, dtype=jnp.int32)) % NZ)
    far = pick(zag, ((1 - zh) * NZ + zl)[None]).reshape(n, n)
    others, far, vg1, acc = tie(others, far, vg1, acc)

    far_t = lax.all_gather(far, YC, tiled=True)
    o1, o3 = shift(others, "x", NX, 1), shift(others, "x", NX, -1)
    vg2, vh1 = around(mine(vg1)), swap(vg1)
    vh2 = swap(vg2)
    qlab = jnp.repeat(lax.dynamic_slice_in_dim(vir, (zl * NX + x) * tiles, tiles), TILE)[None, :]
    ids = lambda d, at: jnp.concatenate([(zl + d + jnp.arange(NZ, dtype=jnp.int32)) % NZ, at, ys, c[None]])
    vs = (v_pair, vg1, vh1, vg2, vh2)
    acc = particle_part(ids(0, xs), vir, qlab, (t[None], x1[None], x3[None], x2[None]), vs, acc)
    o1, o3, acc = tie(o1, o3, acc)

    o2 = (shift(o1[:, :half], "x", NX, 1), shift(o3[:, half:], "x", NX, -1))
    acc = particle_part(ids(1, xs), vir, qlab, (others, o1, o3), vs, acc)
    acc = far_part(jnp.stack([1 - zh, o]), occ, klab, w, far_t, acc)
    energies = (occ_energy[None, :], vir_energy[:, None])
    return particle_part(ids(1, xs[::-1]), vir, qlab, o2, vs, acc, True, energies)


def solution(mesh):
    fine = Mesh(mesh.devices.reshape(2, NY, NC, NZ, NX), AXES)
    placed = (P(OCC, VIR), P(OCC, None), P(VIR, None), P(), P(), P(OCC), P(VIR))
    return jax.shard_map(
        per_device, mesh=fine, in_specs=placed, out_specs=P(VIR, OCC), check_vma=False
    )
```

time: 213 us -> 174 us (0.82)
  blocking collectives: 30.5 us -> 0 us
  waiting for transfers between devices: 81.7 us -> 61.5 us
  Pallas kernels: 30.4 us -> 41.8 us
  starting transfers between devices: 40.3 us -> 36.8 us
    ppermute x23 -> x8, waiting for transfers between devices: 80.8 us -> 33.2 us  [shift(): return lax.ppermute(a, axis, ring(n, d))]
    all_to_all x1 -> x0, blocking collectives: 30.5 us -> none  [per_device(): lax.all_to_all(v_rows, VIR, 1, 0, tiled=True).reshape(NZ * NX, TILE, n)]
    ppermute x23 -> x8, starting transfers between devices: 40.1 us -> 11.1 us  [shift(): return lax.ppermute(a, axis, ring(n, d))]
    ppermute x0 -> x10, starting transfers between devices: none -> 17.5 us  [the longest x6 13.4 us: swap(): return lax.ppermute(a, 'c', ring(NC, 1))]
    ppermute x0 -> x10, waiting for transfers between devices: none -> 17.2 us  [the longest x4 13 us: around(): return lax.ppermute(a, YC, AROUND)]
    pallas_call x4 -> x6, Pallas kernels: 18.6 us -> 33.7 us  [the longest x3 20.3 us: particle_part(): pl.pallas_call(functools.partial(particle_kernel, count=count, split=spli...]
    all_to_all x0 -> x1, starting transfers between devices: none -> 8.18 us  [per_device(): lax.all_to_all(v_rows, VIR, 1, 0, tiled=True).reshape(NZ * NX, TILE, n)]
    all_gather x4 -> x2, waiting for transfers between devices: 0.08 us -> 6.22 us  [the longest x1 6.22 us: per_device(): zag = lax.all_gather(t, z)]
  transfers between devices with their start and end apart: 27 -> 21, of which waited for: 12 -> 11; matrix products, arithmetic and copies ran while one was open for 5% -> 9% of each run, Pallas kernels for 12% -> 21%
where the time goes in v2:
time: 174 us; the launch traced here: 173 us
  waiting for transfers between devices  61.5 us (35%)
  Pallas kernels  41.8 us (24%)
  starting transfers between devices  36.8 us (21%)
  between operations  13.6 us (8%)
  local copies, waits for them, and re-layouts  10.7 us (6%)
  other arithmetic  8.89 us (5%)
    ppermute x8, waiting for transfers between devices, shift(): return lax.ppermute(a, axis, ring(n, d))  33.2 us
    pallas_call x3, Pallas kernels, particle_part(): pl.pallas_call(functools.partial(particle_kernel, count=count, split=spli...  20.3 us
    ppermute x6, starting transfers between devices, swap(): return lax.ppermute(a, 'c', ring(NC, 1))  13.4 us
    ppermute x4, waiting for transfers between devices, around(): return lax.ppermute(a, YC, AROUND)  13 us
    ppermute x8, starting transfers between devices, shift(): return lax.ppermute(a, axis, ring(n, d))  11.1 us
    all_to_all x1, starting transfers between devices, per_device(): lax.all_to_all(v_rows, VIR, 1, 0, tiled=True).reshape(NZ * NX, TILE, n)  8.18 us
    pallas_call x1, Pallas kernels, hole_part(): pl.pallas_call(functools.partial(hole_kernel, has_acc=acc is not None), o...  8.02 us
    pallas_call x1, Pallas kernels, far_part(): pl.pallas_call(far_kernel, out_shape=jax.ShapeDtypeStruct((n, n), F32), g...  7.49 us
  transfers between devices with their start and end apart: 21, of which 11 were waited for; matrix products, arithmetic and copies ran while one was open for 9% of the time, Pallas kernels for 21%

profile of v2, /device:TPU:1, one launch (start us, length us, event | category | flops | bytes accessed | tf_op | source)
XLA Modules:
  0.0 173.3 jit_solution(494278908056646669)
XLA Ops:
  7.3 3.3 %collective-permute-start.2 = (bf16[512,512]{1,0:T(8,128)(2,1)}, bf16[512,512]{1,0:T(8,128)(2,1)S(1)}, u32[]{:S(2)}, u32[]{:S(2)}) collective-permute-start(bf16[512,512]{1,0:T(8,128)(2,1)} %param.8), channel_id=1, source_target_pairs={{0,16},{16,0},{1,17},{17,1},{2,18},{18,2},{3,19},{19,3},{4,20},{20... | collective-permute-start | bytes 1572872 | tf_op jit(solution)/shard_map/ppermute | solution.py:246
  10.6 1.7 %collective-permute-done.2 = bf16[512,512]{1,0:T(8,128)(2,1)S(1)} collective-permute-done((bf16[512,512]{1,0:T(8,128)(2,1)}, bf16[512,512]{1,0:T(8,128)(2,1)S(1)}, u32[]{:S(2)}, u32[]{:S(2)}) %collective-permute-start.2) | collective-permute-done | bytes 524320 | tf_op jit(solution)/shard_map/ppermute | solution.py:246
  17.2 8.2 %all-to-all-start = ((bf16[64,16,512]{2,0,1:T(8,128)(2,1)}), bf16[64,16,512]{2,0,1:T(8,128)(2,1)S(1)}, u32[]{:S(2)}, u32[]{:S(2)}) async-start(bf16[64,16,512]{2,0,1:T(8,128)(2,1)} %bitcast.31), calls=%async_computation | async-start | bytes 2097152 | tf_op jit(solution)/shard_map/all_to_all | solution.py:267
  28.2 21.5 %collective-permute-done = bf16[512,512]{1,0:T(8,128)(2,1)S(1)} collective-permute-done((bf16[512,512]{1,0:T(8,128)(2,1)S(1)}, bf16[512,512]{1,0:T(8,128)(2,1)S(1)}, u32[]{:S(2)}, u32[]{:S(2)}) %collective-permute-start) | collective-permute-done | bytes 524320 | tf_op jit(solution)/shard_map/ppermute | solution.py:23
  52.5 2.7 %collective-permute-start.5 = (bf16[256,512]{1,0:T(8,128)(2,1)S(1)}, bf16[256,512]{1,0:T(8,128)(2,1)}, u32[]{:S(2)}, u32[]{:S(2)}) collective-permute-start(bf16[256,512]{1,0:T(8,128)(2,1)S(1)} %slice.25), channel_id=1, source_target_pairs={{0,3},{1,0},{2,1},{3,2},{4,7},{5,4},{6,5},{7,6},{8,11},{9,8},{10,9... | collective-permute-start | bytes 786440 | tf_op jit(solution)/shard_map/ppermute | solution.py:23
  55.2 6.5 %collective-permute-done.4 = bf16[256,512]{1,0:T(8,128)(2,1)S(1)} collective-permute-done((bf16[256,512]{1,0:T(8,128)(2,1)S(1)}, bf16[256,512]{1,0:T(8,128)(2,1)S(1)}, u32[]{:S(2)}, u32[]{:S(2)}) %collective-permute-start.4) | collective-permute-done | bytes 262176 | tf_op jit(solution)/shard_map/ppermute | solution.py:23
  61.8 4.1 %all-to-all-done = bf16[64,16,512]{2,0,1:T(8,128)(2,1)S(1)} async-done(((bf16[64,16,512]{2,0,1:T(8,128)(2,1)}), bf16[64,16,512]{2,0,1:T(8,128)(2,1)S(1)}, u32[]{:S(2)}, u32[]{:S(2)}) %all-to-all-start) | async-done | bytes 1048608 | tf_op jit(solution)/shard_map/all_to_all | solution.py:267
  66.4 2.3 %collective-permute-done.8 = bf16[16,64,512]{2,1,0:T(8,128)(2,1)S(1)} collective-permute-done((bf16[16,64,512]{2,1,0:T(8,128)(2,1)S(1)}, bf16[16,64,512]{2,1,0:T(8,128)(2,1)S(1)}, u32[]{:S(2)}, u32[]{:S(2)}) %collective-permute-start.8) | collective-permute-done | bytes 1048608 | tf_op jit(solution)/shard_map/ppermute | solution.py:246
  72.8 8.0 %hole_part.1.refs_9_ = f32[512,512]{1,0:T(8,128)} custom-call(s32[6]{0:T(128)} %pad_add_fusion.idx, s32[128]{0:T(128)} %occ.3, s32[1,8192]{1,0:T(1,128)} %broadcast_in_dim_reshape.7.klab, bf16[512,8192]{1,0:T(8,128)(2,1)} %w.3, bf16[1024,512]{1,0:T(8,128)(2,1)} %bitcast.39, bf16[1024,512]{1,0:T(8,128)(2,1)} %bitcast.16.g1, bf16[1024,512]{1,0:T(8,128)(2,1)} %bitcast.44, ...), custom_call_target="tpu_custom_call" | custom-call | flops 2147483648 | bytes 9437184 | tf_op jit(solution)/shard_map/hole_part/pallas_call | solution.py:106
  80.8 6.2 %all-gather.6.cloned.1.call-done = bf16[4096,512]{1,0:T(8,128)(2,1)} async-done(((bf16[512,512]{1,0:T(8,128)(2,1)}), bf16[4096,512]{1,0:T(8,128)(2,1)}) %all-gather.6.cloned.1.call-update) | async-done | bytes 4194320 | tf_op jit(solution)/shard_map/all_gather | solution.py:265
  87.0 4.1 %pick.2.refs_0_ = bf16[3,512,512]{2,1,0:T(8,128)(2,1)} custom-call(s32[3]{0:T(128)} %fusion.1.idx, bf16[8,512,512]{2,1,0:T(8,128)(2,1)} %bitcast.32), custom_call_target="tpu_custom_call" | custom-call | tf_op jit(solution)/shard_map/pick/pallas_call | solution.py:228
  91.1 1.9 %pick.3 = bf16[1,512,512]{2,1,0:T(8,128)(2,1)} custom-call(s32[1]{0:T(128)} %bitcast.6.idx, bf16[8,512,512]{2,1,0:T(8,128)(2,1)} %bitcast.33), custom_call_target="tpu_custom_call" | custom-call | tf_op jit(solution)/shard_map/pick/pallas_call | solution.py:228
  94.4 1.7 select_bitcast_fusion
  96.1 1.7 collective-permute-start.14
  99.2 2.4 %collective-permute-start.12 = (bf16[3,512,512]{2,1,0:T(8,128)(2,1)}, bf16[3,512,512]{2,1,0:T(8,128)(2,1)}, u32[]{:S(2)}, u32[]{:S(2)}) collective-permute-start(bf16[3,512,512]{2,1,0:T(8,128)(2,1)} %pick.2.refs_0_), channel_id=1, source_target_pairs={{0,3},{1,0},{2,1},{3,2},{4,7},{5,4},{6,5},{7,6},{8,11},{9,8},{10,9... | collective-permute-start | bytes 4718600 | tf_op jit(solution)/shard_map/ppermute | solution.py:23
  101.6 11.6 %collective-permute-done.14.refs_7_.refs_6_.refs_5_ = bf16[16,64,512]{2,1,0:T(8,128)(2,1)S(1)} collective-permute-done((bf16[16,64,512]{2,1,0:T(8,128)(2,1)S(1)}, bf16[16,64,512]{2,1,0:T(8,128)(2,1)S(1)}, u32[]{:S(2)}, u32[]{:S(2)}) %collective-permute-start.14) | collective-permute-done | bytes 1048608 | tf_op jit(solution)/shard_map/ppermute | solution.py:250
  113.1 8.4 %collective-permute-start.15 = (bf16[16,64,512]{2,1,0:T(8,128)(2,1)S(1)}, bf16[16,64,512]{2,1,0:T(8,128)(2,1)}, u32[]{:S(2)}, u32[]{:S(2)}) collective-permute-start(bf16[16,64,512]{2,1,0:T(8,128)(2,1)S(1)} %collective-permute-done.14.refs_7_.refs_6_.refs_5_), channel_id=1, source_target_pairs={{0,16},{16,0},{1,17},{17,1},{2,18},{18,2},{3,19},{19,3},{4,20},{20... | collective-permute-start | bytes 3145736 | tf_op jit(solution)/shard_map/ppermute | solution.py:246
  123.2 1.8 %maximum_bitcast_fusion.refs_3_ = bf16[1,512,512]{2,1,0:T(8,128)(2,1)} fusion(bf16[256,512]{1,0:T(8,128)(2,1)} %collective-permute-done.5, bf16[256,512]{1,0:T(8,128)(2,1)S(1)} %collective-permute-done.4), kind=kLoop, calls=%fused_computation.4 | loop fusion | flops 1048576 | bytes 1048576 | tf_op jit(solution)/shard_map/broadcast_in_dim | solution.py:300
  126.3 5.6 %particle_part.2.refs_8_ = f32[512,512]{1,0:T(8,128)} custom-call(s32[13]{0:T(128)} %get-tuple-element.38.idx, s32[128]{0:T(128)} %vir.5, s32[1,512]{1,0:T(1,128)} %broadcast_in_dim_reshape.6.qlab, bf16[1,512,512]{2,1,0:T(8,128)(2,1)} %bitcast.35, bf16[1,512,512]{2,1,0:T(8,128)(2,1)} %bitcast.41, bf16[1,512,512]{2,1,0:T(8,128)(2,1)} %bitcast.42, ...), custom_call_target="tpu_custom_call" | custom-call | flops 1073741824 | bytes 5242880 | tf_op jit(solution)/shard_map/particle_part/pallas_call | solution.py:206
  131.9 4.4 %collective-permute-done.11.refs_1_ = bf16[3,512,512]{2,1,0:T(8,128)(2,1)} collective-permute-done((bf16[3,512,512]{2,1,0:T(8,128)(2,1)}, bf16[3,512,512]{2,1,0:T(8,128)(2,1)}, u32[]{:S(2)}, u32[]{:S(2)}) %collective-permute-start.11) | collective-permute-done | bytes 1572896 | tf_op jit(solution)/shard_map/ppermute | solution.py:23
  138.8 2.7 %collective-permute-start.17 = (bf16[3,256,512]{2,1,0:T(8,128)(2,1)S(1)}, bf16[3,256,512]{2,1,0:T(8,128)(2,1)S(1)}, u32[]{:S(2)}, u32[]{:S(2)}) collective-permute-start(bf16[3,256,512]{2,1,0:T(8,128)(2,1)S(1)} %slice.31), channel_id=1, source_target_pairs={{0,3},{1,0},{2,1},{3,2},{4,7},{5,4},{6,5},{7,6},{8,11},{9,8},{10,9... | collective-permute-start | bytes 2359304 | tf_op jit(solution)/shard_map/ppermute | solution.py:23
  143.0 8.6 %particle_part.3.acc = f32[512,512]{1,0:T(8,128)} custom-call(s32[13]{0:T(128)} %get-tuple-element.37.idx, s32[128]{0:T(128)} %vir.5, s32[1,512]{1,0:T(1,128)} %broadcast_in_dim_reshape.6.qlab, bf16[3,512,512]{2,1,0:T(8,128)(2,1)} %pick.2.refs_0_, bf16[3,512,512]{2,1,0:T(8,128)(2,1)} %collective-permute-done.11.refs_1_, ...), custom_call_target="tpu_custom_call" | custom-call | flops 2415919104 | bytes 10485760 | tf_op jit(solution)/shard_map/particle_part/pallas_call | solution.py:206
  151.6 7.5 %far_part.1.refs_7_ = f32[512,512]{1,0:T(8,128)} custom-call(s32[2]{0:T(128)} %pad_add_fusion.1.idx, s32[128]{0:T(128)} %occ.3, s32[1,8192]{1,0:T(1,128)} %broadcast_in_dim_reshape.7.klab, bf16[512,8192]{1,0:T(8,128)(2,1)} %w.3, bf16[4096,512]{1,0:T(8,128)(2,1)} %all-gather.4.cloned.1.call-done.t, f32[512,512]{1,0:T(8,128)} %particle_part.3.acc), custom_call_target="tpu_custom_call" | custom-call | flops 2147483648 | bytes 9437184 | tf_op jit(solution)/shard_map/far_part/pallas_call | solution.py:126
  160.3 6.1 %particle_last.1 = f32[512,512]{1,0:T(8,128)} custom-call(s32[13]{0:T(128)} %get-tuple-element.39.idx, s32[128]{0:T(128)} %vir.5, s32[1,512]{1,0:T(1,128)} %broadcast_in_dim_reshape.6.qlab, bf16[3,256,512]{2,1,0:T(8,128)(2,1)} %copy-done.8, bf16[3,256,512]{2,1,0:T(8,128)(2,1)} %copy-done.9, bf16[2,16,64,512]{3,2,1,0:T(8,128)(2,1)} %copy-done, ...), custom_call_target="tpu_custom_call" | custom-call | flops 805306368 | bytes 4194304 | tf_op jit(solution)/shard_map/particle_last/pallas_call | solution.py:206
  (81 shorter events, 26.6 us)
Async XLA Ops:
  6.5 80.5 %all-gather.6.cloned.1.call-start = ((), (), s32[]{:S(2)}) async-start(), calls=%async_computation.2 | async-start | bytes 4718592 | tf_op jit(solution)/shard_map/all_gather | solution.py:265
  7.3 5.1 %collective-permute-start.2 = (bf16[512,512]{1,0:T(8,128)(2,1)}, bf16[512,512]{1,0:T(8,128)(2,1)S(1)}, u32[]{:S(2)}, u32[]{:S(2)}) collective-permute-start(bf16[512,512]{1,0:T(8,128)(2,1)} %param.8), channel_id=1, source_target_pairs={{0,16},{16,0},{1,17},{17,1},{2,18},{18,2},{3,19},{19,3},{4,20},{20... | collective-permute-start | bytes 1572872 | tf_op jit(solution)/shard_map/ppermute | solution.py:246
  13.7 36.7 %collective-permute-start.3 = (bf16[2,512,512]{2,1,0:T(8,128)(2,1)S(1)}, bf16[2,512,512]{2,1,0:T(8,128)(2,1)}, u32[]{:S(2)}, u32[]{:S(2)}) collective-permute-start(bf16[2,512,512]{2,1,0:T(8,128)(2,1)S(1)} %maximum_select_fusion.1), channel_id=1, source_target_pairs={{0,32},{16,112},{32,64},{48,16},{64,96},{80,48},{96,0},{112,80},{1... | collective-permute-start | bytes 3145736 | tf_op jit(solution)/shard_map/ppermute | solution.py:250
  17.2 48.7 %all-to-all-start = ((bf16[64,16,512]{2,0,1:T(8,128)(2,1)}), bf16[64,16,512]{2,0,1:T(8,128)(2,1)S(1)}, u32[]{:S(2)}, u32[]{:S(2)}) async-start(bf16[64,16,512]{2,0,1:T(8,128)(2,1)} %bitcast.31), calls=%async_computation | async-start | bytes 2097152 | tf_op jit(solution)/shard_map/all_to_all | solution.py:267
  25.4 126.2 %all-gather.4.cloned.1.call-start = ((), (), s32[]{:S(2)}) async-start(), calls=%async_computation.1 | async-start | bytes 4718592 | tf_op jit(solution)/shard_map/all_gather | solution.py:293
  25.4 24.3 %collective-permute-start = (bf16[512,512]{1,0:T(8,128)(2,1)S(1)}, bf16[512,512]{1,0:T(8,128)(2,1)S(1)}, u32[]{:S(2)}, u32[]{:S(2)}) collective-permute-start(bf16[512,512]{1,0:T(8,128)(2,1)S(1)} %copy-done.3), channel_id=1, source_target_pairs={{0,1},{1,2},{2,3},{3,0},{4,5},{5,6},{6,7},{7,4},{8,9},{9,10},{10,1... | collective-permute-start | bytes 1572872 | tf_op jit(solution)/shard_map/ppermute | solution.py:23
  26.9 23.6 %collective-permute-start.1 = (bf16[512,512]{1,0:T(8,128)(2,1)S(1)}, bf16[512,512]{1,0:T(8,128)(2,1)S(1)}, u32[]{:S(2)}, u32[]{:S(2)}) collective-permute-start(bf16[512,512]{1,0:T(8,128)(2,1)S(1)} %copy-done.3), channel_id=1, source_target_pairs={{0,3},{1,0},{2,1},{3,2},{4,7},{5,4},{6,5},{7,6},{8,11},{9,8},{10,9... | collective-permute-start | bytes 1572872 | tf_op jit(solution)/shard_map/ppermute | solution.py:23
  49.7 19.0 %copy-start.5 = (bf16[512,512]{1,0:T(8,128)(2,1)}, bf16[512,512]{1,0:T(8,128)(2,1)S(1)}, u32[]{:S(2)}) copy-start(bf16[512,512]{1,0:T(8,128)(2,1)S(1)} %collective-permute-done) | copy-start | bytes 1572868
  50.4 15.4 %collective-permute-start.7 = (bf16[2,512,512]{2,1,0:T(8,128)(2,1)}, bf16[2,512,512]{2,1,0:T(8,128)(2,1)S(1)}, u32[]{:S(2)}, u32[]{:S(2)}) collective-permute-start(bf16[2,512,512]{2,1,0:T(8,128)(2,1)} %collective-permute-done.3), channel_id=1, source_target_pairs={{0,16},{16,0},{1,17},{17,1},{2,18},{18,2},{3,19},{19,3},{4,20},{20... | collective-permute-start | bytes 3145736 | tf_op jit(solution)/shard_map/ppermute | solution.py:246
  51.9 14.0 %collective-permute-start.6 = (bf16[512,512]{1,0:T(8,128)(2,1)S(1)}, bf16[512,512]{1,0:T(8,128)(2,1)}, u32[]{:S(2)}, u32[]{:S(2)}) collective-permute-start(bf16[512,512]{1,0:T(8,128)(2,1)S(1)} %select_bitcast_fusion.1), channel_id=1, source_target_pairs={{0,32},{16,112},{32,64},{48,16},{64,96},{80,48},{96,0},{112,80},{1... | collective-permute-start | bytes 1572872 | tf_op jit(solution)/shard_map/ppermute | solution.py:250
  52.4 9.4 %collective-permute-start.4 = (bf16[256,512]{1,0:T(8,128)(2,1)S(1)}, bf16[256,512]{1,0:T(8,128)(2,1)S(1)}, u32[]{:S(2)}, u32[]{:S(2)}) collective-permute-start(bf16[256,512]{1,0:T(8,128)(2,1)S(1)} %slice.24), channel_id=1, source_target_pairs={{0,1},{1,2},{2,3},{3,0},{4,5},{5,6},{6,7},{7,4},{8,9},{9,10},{10,1... | collective-permute-start | bytes 786440 | tf_op jit(solution)/shard_map/ppermute | solution.py:23
  52.5 9.3 %collective-permute-start.5 = (bf16[256,512]{1,0:T(8,128)(2,1)S(1)}, bf16[256,512]{1,0:T(8,128)(2,1)}, u32[]{:S(2)}, u32[]{:S(2)}) collective-permute-start(bf16[256,512]{1,0:T(8,128)(2,1)S(1)} %slice.25), channel_id=1, source_target_pairs={{0,3},{1,0},{2,1},{3,2},{4,7},{5,4},{6,5},{7,6},{8,11},{9,8},{10,9... | collective-permute-start | bytes 786440 | tf_op jit(solution)/shard_map/ppermute | solution.py:23
  65.9 2.8 %collective-permute-start.8 = (bf16[16,64,512]{2,1,0:T(8,128)(2,1)S(1)}, bf16[16,64,512]{2,1,0:T(8,128)(2,1)S(1)}, u32[]{:S(2)}, u32[]{:S(2)}) collective-permute-start(bf16[16,64,512]{2,1,0:T(8,128)(2,1)S(1)} %bitcast.36), channel_id=1, source_target_pairs={{0,16},{16,0},{1,17},{17,1},{2,18},{18,2},{3,19},{19,3},{4,20},{20... | collective-permute-start | bytes 3145736 | tf_op jit(solution)/shard_map/ppermute | solution.py:246
  69.0 25.4 %collective-permute-start.9 = (bf16[2,16,64,512]{3,2,1,0:T(8,128)(2,1)S(1)}, bf16[2,16,64,512]{3,2,1,0:T(8,128)(2,1)}, u32[]{:S(2)}, u32[]{:S(2)}) collective-permute-start(bf16[2,16,64,512]{3,2,1,0:T(8,128)(2,1)S(1)} %maximum_select_fusion.refs_4_.refs_3_.refs_2_), channel_id=1, source_target_pairs={{0,32},{16,112},{32,64},{48,16},{64,96},{80,48},{96,0},{112,80},{1... | collective-permute-start | bytes 6291464 | tf_op jit(solution)/shard_map/ppermute | solution.py:250
  69.8 2.1 %collective-permute-start.10 = (bf16[512,512]{1,0:T(8,128)(2,1)}, bf16[512,512]{1,0:T(8,128)(2,1)S(1)}, u32[]{:S(2)}, u32[]{:S(2)}) collective-permute-start(bf16[512,512]{1,0:T(8,128)(2,1)} %collective-permute-done.6.g2), channel_id=1, source_target_pairs={{0,16},{16,0},{1,17},{17,1},{2,18},{18,2},{3,19},{19,3},{4,20},{20... | collective-permute-start | bytes 1572872 | tf_op jit(solution)/shard_map/ppermute | solution.py:246
  93.0 28.6 %copy-start.14 = (s32[4]{0:T(128)S(1)}, s32[4]{0:T(128)}, u32[]{:S(2)}) copy-start(s32[4]{0:T(128)} %constant.79.clone) | copy-start | bytes 52
  93.0 28.7 %copy-start.12 = (s32[128]{0:T(128)S(1)}, s32[128]{0:T(128)}, u32[]{:S(2)}) copy-start(s32[128]{0:T(128)} %vir.5) | copy-start | bytes 1540
  96.1 17.1 %collective-permute-start.14 = (bf16[16,64,512]{2,1,0:T(8,128)(2,1)S(1)}, bf16[16,64,512]{2,1,0:T(8,128)(2,1)S(1)}, u32[]{:S(2)}, u32[]{:S(2)}) collective-permute-start(bf16[16,64,512]{2,1,0:T(8,128)(2,1)S(1)} %select_bitcast_fusion), channel_id=1, source_target_pairs={{0,32},{16,112},{32,64},{48,16},{64,96},{80,48},{96,0},{112,80},{1... | collective-permute-start | bytes 3145736 | tf_op jit(solution)/shard_map/ppermute | solution.py:250
  97.8 27.1 %collective-permute-start.13 = (bf16[2,16,64,512]{3,2,1,0:T(8,128)(2,1)}, bf16[2,16,64,512]{3,2,1,0:T(8,128)(2,1)S(1)}, u32[]{:S(2)}, u32[]{:S(2)}) collective-permute-start(bf16[2,16,64,512]{3,2,1,0:T(8,128)(2,1)} %collective-permute-done.9.refs_5_.refs_4_.refs_3_), channel_id=1, source_target_pairs={{0,16},{16,0},{1,17},{17,1},{2,18},{18,2},{3,19},{19,3},{4,20},{20... | collective-permute-start | bytes 6291464 | tf_op jit(solution)/shard_map/ppermute | solution.py:246
  98.9 37.5 %collective-permute-start.11 = (bf16[3,512,512]{2,1,0:T(8,128)(2,1)}, bf16[3,512,512]{2,1,0:T(8,128)(2,1)}, u32[]{:S(2)}, u32[]{:S(2)}) collective-permute-start(bf16[3,512,512]{2,1,0:T(8,128)(2,1)} %pick.2.refs_0_), channel_id=1, source_target_pairs={{0,1},{1,2},{2,3},{3,0},{4,5},{5,6},{6,7},{7,4},{8,9},{9,10},{10,1... | collective-permute-start | bytes 4718600 | tf_op jit(solution)/shard_map/ppermute | solution.py:23
  99.2 37.2 %collective-permute-start.12 = (bf16[3,512,512]{2,1,0:T(8,128)(2,1)}, bf16[3,512,512]{2,1,0:T(8,128)(2,1)}, u32[]{:S(2)}, u32[]{:S(2)}) collective-permute-start(bf16[3,512,512]{2,1,0:T(8,128)(2,1)} %pick.2.refs_0_), channel_id=1, source_target_pairs={{0,3},{1,0},{2,1},{3,2},{4,7},{5,4},{6,5},{7,6},{8,11},{9,8},{10,9... | collective-permute-start | bytes 4718600 | tf_op jit(solution)/shard_map/ppermute | solution.py:23
  113.1 11.8 %collective-permute-start.15 = (bf16[16,64,512]{2,1,0:T(8,128)(2,1)S(1)}, bf16[16,64,512]{2,1,0:T(8,128)(2,1)}, u32[]{:S(2)}, u32[]{:S(2)}) collective-permute-start(bf16[16,64,512]{2,1,0:T(8,128)(2,1)S(1)} %collective-permute-done.14.refs_7_.refs_6_.refs_5_), channel_id=1, source_target_pairs={{0,16},{16,0},{1,17},{17,1},{2,18},{18,2},{3,19},{19,3},{4,20},{20... | collective-permute-start | bytes 3145736 | tf_op jit(solution)/shard_map/ppermute | solution.py:246
  137.6 21.6 %collective-permute-start.16 = (bf16[3,256,512]{2,1,0:T(8,128)(2,1)S(1)}, bf16[3,256,512]{2,1,0:T(8,128)(2,1)S(1)}, u32[]{:S(2)}, u32[]{:S(2)}) collective-permute-start(bf16[3,256,512]{2,1,0:T(8,128)(2,1)S(1)} %slice.30), channel_id=1, source_target_pairs={{0,1},{1,2},{2,3},{3,0},{4,5},{5,6},{6,7},{7,4},{8,9},{9,10},{10,1... | collective-permute-start | bytes 2359304 | tf_op jit(solution)/shard_map/ppermute | solution.py:23
  138.8 20.3 %collective-permute-start.17 = (bf16[3,256,512]{2,1,0:T(8,128)(2,1)S(1)}, bf16[3,256,512]{2,1,0:T(8,128)(2,1)S(1)}, u32[]{:S(2)}, u32[]{:S(2)}) collective-permute-start(bf16[3,256,512]{2,1,0:T(8,128)(2,1)S(1)} %slice.31), channel_id=1, source_target_pairs={{0,3},{1,0},{2,1},{3,2},{4,7},{5,4},{6,5},{7,6},{8,11},{9,8},{10,9... | collective-permute-start | bytes 2359304 | tf_op jit(solution)/shard_map/ppermute | solution.py:23
  (12 other events, 65.6 us)
Sparse Core Ops, SparseCore 0:
  9.1 77.8 all-gather.5
  94.5 38.2 all-gather.3

commit v3 on v2

--- a/solution.py
+++ b/solution.py
@@ -264,9 +264,11 @@
 
     zag = lax.all_gather(t, z)
     v_rows = lax.dynamic_slice_in_dim(v, (y * NC + c) * TILE, TILE)
-    v_own = lax.all_to_all(v_rows, VIR, 1, 0, tiled=True).reshape(NZ * NX, TILE, n)
-    x1, x3 = shift(t, "x", NX, 1), shift(t, "x", NX, -1)
-    pair = both(t, swap(t))
+    v_rows = jnp.swapaxes(v_rows.reshape(TILE, NZ * NX, n), 0, 1)
+    v_rows, t0 = tie(v_rows, t)
+    v_own = lax.all_to_all(v_rows, VIR, 0, 0, tiled=True)
+    x1, x3 = shift(t0, "x", NX, 1), shift(t0, "x", NX, -1)
+    pair = both(t0, swap(t0))
     g1 = around(pair)
     x1, x3, g1 = tie(x1, x3, g1)
     x2a, x2b = shift(x1[:half], "x", NX, 1), shift(x3[half:], "x", NX, -1)

time: 174 us -> 172 us (0.989)
    ppermute x4, waiting for transfers between devices: 13 us -> 9.39 us  [around(): return lax.ppermute(a, YC, AROUND)]
    ppermute x6, starting transfers between devices: 13.4 us -> 16.5 us  [swap(): return lax.ppermute(a, 'c', ring(NC, 1))]
    ppermute x4, starting transfers between devices: 4.08 us -> 2.3 us  [around(): return lax.ppermute(a, YC, AROUND)]
    all_gather x1, waiting for transfers between devices: 6.22 us -> 7.99 us  [per_device(): zag = lax.all_gather(t, z)]
  transfers between devices with their start and end apart: 21 -> 21, of which waited for: 11 -> 10; matrix products, arithmetic and copies ran while one was open for 9% -> 9% of each run, Pallas kernels for 21% -> 21%
where the time goes in v3:
time: 172 us
  waiting for transfers between devices  59.9 us (35%)
  Pallas kernels  41.7 us (24%)
  starting transfers between devices  38.1 us (22%)
  between operations  13.6 us (8%)
  local copies, waits for them, and re-layouts  10.8 us (6%)
  other arithmetic  7.57 us (4%)
    ppermute x8, waiting for transfers between devices, shift(): return lax.ppermute(a, axis, ring(n, d))  33.2 us
    pallas_call x3, Pallas kernels, particle_part(): pl.pallas_call(functools.partial(particle_kernel, count=count, split=spli...  20.3 us
    ppermute x6, starting transfers between devices, swap(): return lax.ppermute(a, 'c', ring(NC, 1))  16.5 us
    ppermute x8, starting transfers between devices, shift(): return lax.ppermute(a, axis, ring(n, d))  11.1 us
    ppermute x4, waiting for transfers between devices, around(): return lax.ppermute(a, YC, AROUND)  9.39 us
    all_to_all x1, starting transfers between devices, per_device(): v_own = lax.all_to_all(v_rows, VIR, 0, 0, tiled=True)  8.18 us
    pallas_call x1, Pallas kernels, hole_part(): pl.pallas_call(functools.partial(hole_kernel, has_acc=acc is not None), o...  8 us
    all_gather x1, waiting for transfers between devices, per_device(): zag = lax.all_gather(t, z)  7.99 us
  transfers between devices with their start and end apart: 21, of which 10 were waited for; matrix products, arithmetic and copies ran while one was open for 9% of the time, Pallas kernels for 21%

profile of v3, /device:TPU:1, one launch (start us, length us, event | category | flops | bytes accessed | tf_op | source)
XLA Modules:
  0.0 171.7 jit_solution(6932419445617572752)
XLA Ops:
  9.7 3.2 %collective-permute-start.2 = (bf16[512,512]{1,0:T(8,128)(2,1)S(1)}, bf16[512,512]{1,0:T(8,128)(2,1)S(1)}, u32[]{:S(2)}, u32[]{:S(2)}) collective-permute-start(bf16[512,512]{1,0:T(8,128)(2,1)S(1)} %copy-done.3), channel_id=1, source_target_pairs={{0,16},{16,0},{1,17},{17,1},{2,18},{18,2},{3,19},{19,3},{4,20},{20... | collective-permute-start | bytes 1572872 | tf_op jit(solution)/shard_map/ppermute | solution.py:246
  13.0 1.5 collective-permute-done.2
  15.8 8.2 %all-to-all-start = ((bf16[16,64,512]{2,1,0:T(8,128)(2,1)}), bf16[16,64,512]{2,1,0:T(8,128)(2,1)S(1)}, u32[]{:S(2)}, u32[]{:S(2)}) async-start(bf16[16,64,512]{2,1,0:T(8,128)(2,1)} %bitcast.34), calls=%async_computation | async-start | bytes 2097152 | tf_op jit(solution)/shard_map/all_to_all | solution.py:269
  26.8 21.6 %collective-permute-done = bf16[512,512]{1,0:T(8,128)(2,1)S(1)} collective-permute-done((bf16[512,512]{1,0:T(8,128)(2,1)S(1)}, bf16[512,512]{1,0:T(8,128)(2,1)S(1)}, u32[]{:S(2)}, u32[]{:S(2)}) %collective-permute-start) | collective-permute-done | bytes 524320 | tf_op jit(solution)/shard_map/ppermute | solution.py:23
  50.8 2.7 %collective-permute-start.5 = (bf16[256,512]{1,0:T(8,128)(2,1)S(1)}, bf16[256,512]{1,0:T(8,128)(2,1)S(1)}, u32[]{:S(2)}, u32[]{:S(2)}) collective-permute-start(bf16[256,512]{1,0:T(8,128)(2,1)S(1)} %slice.25), channel_id=1, source_target_pairs={{0,3},{1,0},{2,1},{3,2},{4,7},{5,4},{6,5},{7,6},{8,11},{9,8},{10,9... | collective-permute-start | bytes 786440 | tf_op jit(solution)/shard_map/ppermute | solution.py:23
  53.6 6.2 %collective-permute-done.4 = bf16[256,512]{1,0:T(8,128)(2,1)S(1)} collective-permute-done((bf16[256,512]{1,0:T(8,128)(2,1)S(1)}, bf16[256,512]{1,0:T(8,128)(2,1)S(1)}, u32[]{:S(2)}, u32[]{:S(2)}) %collective-permute-start.4) | collective-permute-done | bytes 262176 | tf_op jit(solution)/shard_map/ppermute | solution.py:23
  59.7 4.7 %all-to-all-done = bf16[16,64,512]{2,1,0:T(8,128)(2,1)S(1)} async-done(((bf16[16,64,512]{2,1,0:T(8,128)(2,1)}), bf16[16,64,512]{2,1,0:T(8,128)(2,1)S(1)}, u32[]{:S(2)}, u32[]{:S(2)}) %all-to-all-start) | async-done | bytes 1048608 | tf_op jit(solution)/shard_map/all_to_all | solution.py:269
  64.9 2.3 %collective-permute-done.8 = bf16[16,64,512]{2,1,0:T(8,128)(2,1)S(1)} collective-permute-done((bf16[16,64,512]{2,1,0:T(8,128)(2,1)S(1)}, bf16[16,64,512]{2,1,0:T(8,128)(2,1)S(1)}, u32[]{:S(2)}, u32[]{:S(2)}) %collective-permute-start.8) | collective-permute-done | bytes 1048608 | tf_op jit(solution)/shard_map/ppermute | solution.py:246
  70.8 8.0 %hole_part.1.refs_9_ = f32[512,512]{1,0:T(8,128)} custom-call(s32[6]{0:T(128)} %pad_add_fusion.idx, s32[128]{0:T(128)} %occ.3, s32[1,8192]{1,0:T(1,128)} %broadcast_in_dim_reshape.7.klab, bf16[512,8192]{1,0:T(8,128)(2,1)} %w.3, bf16[1024,512]{1,0:T(8,128)(2,1)} %bitcast.41, bf16[1024,512]{1,0:T(8,128)(2,1)} %bitcast.16.g1, bf16[1024,512]{1,0:T(8,128)(2,1)} %bitcast.17.h1, ...), custom_call_target="tpu_custom_call" | custom-call | flops 2147483648 | bytes 9437184 | tf_op jit(solution)/shard_map/hole_part/pallas_call | solution.py:106
  78.8 8.0 %all-gather.6.cloned.1.call-done = bf16[4096,512]{1,0:T(8,128)(2,1)} async-done(((bf16[512,512]{1,0:T(8,128)(2,1)}), bf16[4096,512]{1,0:T(8,128)(2,1)}) %all-gather.6.cloned.1.call-update) | async-done | bytes 4194320 | tf_op jit(solution)/shard_map/all_gather | solution.py:265
  86.8 4.1 %pick.2.refs_0_ = bf16[3,512,512]{2,1,0:T(8,128)(2,1)} custom-call(s32[3]{0:T(128)} %fusion.1.idx, bf16[8,512,512]{2,1,0:T(8,128)(2,1)} %bitcast.35), custom_call_target="tpu_custom_call" | custom-call | tf_op jit(solution)/shard_map/pick/pallas_call | solution.py:228
  90.9 1.9 %pick.3 = bf16[1,512,512]{2,1,0:T(8,128)(2,1)} custom-call(s32[1]{0:T(128)} %bitcast.6.idx, bf16[8,512,512]{2,1,0:T(8,128)(2,1)} %bitcast.36), custom_call_target="tpu_custom_call" | custom-call | tf_op jit(solution)/shard_map/pick/pallas_call | solution.py:228
  92.9 1.7 select_bitcast_fusion
  95.6 1.7 %collective-permute-start.13 = (bf16[2,16,64,512]{3,2,1,0:T(8,128)(2,1)}, bf16[2,16,64,512]{3,2,1,0:T(8,128)(2,1)S(1)}, u32[]{:S(2)}, u32[]{:S(2)}) collective-permute-start(bf16[2,16,64,512]{3,2,1,0:T(8,128)(2,1)} %collective-permute-done.9.refs_5_.refs_4_.refs_3_), channel_id=1, source_target_pairs={{0,16},{16,0},{1,17},{17,1},{2,18},{18,2},{3,19},{19,3},{4,20},{20... | collective-permute-start | bytes 6291464 | tf_op jit(solution)/shard_map/ppermute | solution.py:246
  97.7 2.4 %collective-permute-start.12 = (bf16[3,512,512]{2,1,0:T(8,128)(2,1)}, bf16[3,512,512]{2,1,0:T(8,128)(2,1)}, u32[]{:S(2)}, u32[]{:S(2)}) collective-permute-start(bf16[3,512,512]{2,1,0:T(8,128)(2,1)} %pick.2.refs_0_), channel_id=1, source_target_pairs={{0,3},{1,0},{2,1},{3,2},{4,7},{5,4},{6,5},{7,6},{8,11},{9,8},{10,9... | collective-permute-start | bytes 4718600 | tf_op jit(solution)/shard_map/ppermute | solution.py:23
  100.1 9.3 %collective-permute-done.14.refs_7_.refs_6_.refs_5_ = bf16[16,64,512]{2,1,0:T(8,128)(2,1)S(1)} collective-permute-done((bf16[16,64,512]{2,1,0:T(8,128)(2,1)S(1)}, bf16[16,64,512]{2,1,0:T(8,128)(2,1)S(1)}, u32[]{:S(2)}, u32[]{:S(2)}) %collective-permute-start.14) | collective-permute-done | bytes 1048608 | tf_op jit(solution)/shard_map/ppermute | solution.py:250
  109.3 10.4 %collective-permute-start.15 = (bf16[16,64,512]{2,1,0:T(8,128)(2,1)S(1)}, bf16[16,64,512]{2,1,0:T(8,128)(2,1)}, u32[]{:S(2)}, u32[]{:S(2)}) collective-permute-start(bf16[16,64,512]{2,1,0:T(8,128)(2,1)S(1)} %collective-permute-done.14.refs_7_.refs_6_.refs_5_), channel_id=1, source_target_pairs={{0,16},{16,0},{1,17},{17,1},{2,18},{18,2},{3,19},{19,3},{4,20},{20... | collective-permute-start | bytes 3145736 | tf_op jit(solution)/shard_map/ppermute | solution.py:246
  121.3 1.8 %maximum_bitcast_fusion.refs_3_ = bf16[1,512,512]{2,1,0:T(8,128)(2,1)} fusion(bf16[256,512]{1,0:T(8,128)(2,1)} %copy-done.10, bf16[256,512]{1,0:T(8,128)(2,1)S(1)} %collective-permute-done.4), kind=kLoop, calls=%fused_computation.4 | loop fusion | flops 1048576 | bytes 1048576 | tf_op jit(solution)/shard_map/broadcast_in_dim | solution.py:302
  124.5 5.7 %particle_part.2.refs_8_ = f32[512,512]{1,0:T(8,128)} custom-call(s32[13]{0:T(128)} %get-tuple-element.42.idx, s32[128]{0:T(128)} %vir.5, s32[1,512]{1,0:T(1,128)} %broadcast_in_dim_reshape.6.qlab, bf16[1,512,512]{2,1,0:T(8,128)(2,1)} %bitcast.37, bf16[1,512,512]{2,1,0:T(8,128)(2,1)} %bitcast.43, bf16[1,512,512]{2,1,0:T(8,128)(2,1)} %bitcast.44, ...), custom_call_target="tpu_custom_call" | custom-call | flops 1073741824 | bytes 5242880 | tf_op jit(solution)/shard_map/particle_part/pallas_call | solution.py:206
  130.1 4.7 %collective-permute-done.11.refs_1_ = bf16[3,512,512]{2,1,0:T(8,128)(2,1)} collective-permute-done((bf16[3,512,512]{2,1,0:T(8,128)(2,1)}, bf16[3,512,512]{2,1,0:T(8,128)(2,1)}, u32[]{:S(2)}, u32[]{:S(2)}) %collective-permute-start.11) | collective-permute-done | bytes 1572896 | tf_op jit(solution)/shard_map/ppermute | solution.py:23
  137.3 2.7 %collective-permute-start.17 = (bf16[3,256,512]{2,1,0:T(8,128)(2,1)S(1)}, bf16[3,256,512]{2,1,0:T(8,128)(2,1)S(1)}, u32[]{:S(2)}, u32[]{:S(2)}) collective-permute-start(bf16[3,256,512]{2,1,0:T(8,128)(2,1)S(1)} %slice.31), channel_id=1, source_target_pairs={{0,3},{1,0},{2,1},{3,2},{4,7},{5,4},{6,5},{7,6},{8,11},{9,8},{10,9... | collective-permute-start | bytes 2359304 | tf_op jit(solution)/shard_map/ppermute | solution.py:23
  141.5 8.6 %particle_part.3.acc = f32[512,512]{1,0:T(8,128)} custom-call(s32[13]{0:T(128)} %get-tuple-element.41.idx, s32[128]{0:T(128)} %vir.5, s32[1,512]{1,0:T(1,128)} %broadcast_in_dim_reshape.6.qlab, bf16[3,512,512]{2,1,0:T(8,128)(2,1)} %pick.2.refs_0_, bf16[3,512,512]{2,1,0:T(8,128)(2,1)} %collective-permute-done.11.refs_1_, ...), custom_call_target="tpu_custom_call" | custom-call | flops 2415919104 | bytes 10485760 | tf_op jit(solution)/shard_map/particle_part/pallas_call | solution.py:206
  150.0 7.5 %far_part.1.refs_7_ = f32[512,512]{1,0:T(8,128)} custom-call(s32[2]{0:T(128)} %pad_add_fusion.1.idx, s32[128]{0:T(128)} %occ.3, s32[1,8192]{1,0:T(1,128)} %broadcast_in_dim_reshape.7.klab, bf16[512,8192]{1,0:T(8,128)(2,1)} %w.3, bf16[4096,512]{1,0:T(8,128)(2,1)} %all-gather.4.cloned.1.call-done.t, f32[512,512]{1,0:T(8,128)} %particle_part.3.acc), custom_call_target="tpu_custom_call" | custom-call | flops 2147483648 | bytes 9437184 | tf_op jit(solution)/shard_map/far_part/pallas_call | solution.py:126
  158.8 6.1 %particle_last.1 = f32[512,512]{1,0:T(8,128)} custom-call(s32[13]{0:T(128)} %get-tuple-element.43.idx, s32[128]{0:T(128)} %vir.5, s32[1,512]{1,0:T(1,128)} %broadcast_in_dim_reshape.6.qlab, bf16[3,256,512]{2,1,0:T(8,128)(2,1)} %copy-done.7, bf16[3,256,512]{2,1,0:T(8,128)(2,1)} %copy-done.8, bf16[2,16,64,512]{3,2,1,0:T(8,128)(2,1)} %copy-done, ...), custom_call_target="tpu_custom_call" | custom-call | flops 805306368 | bytes 4194304 | tf_op jit(solution)/shard_map/particle_last/pallas_call | solution.py:206
  (81 shorter events, 23.2 us)
Async XLA Ops:
  6.5 80.3 %all-gather.6.cloned.1.call-start = ((), (), s32[]{:S(2)}) async-start(), calls=%async_computation.2 | async-start | bytes 4718592 | tf_op jit(solution)/shard_map/all_gather | solution.py:265
  9.7 4.8 %collective-permute-start.2 = (bf16[512,512]{1,0:T(8,128)(2,1)S(1)}, bf16[512,512]{1,0:T(8,128)(2,1)S(1)}, u32[]{:S(2)}, u32[]{:S(2)}) collective-permute-start(bf16[512,512]{1,0:T(8,128)(2,1)S(1)} %copy-done.3), channel_id=1, source_target_pairs={{0,16},{16,0},{1,17},{17,1},{2,18},{18,2},{3,19},{19,3},{4,20},{20... | collective-permute-start | bytes 1572872 | tf_op jit(solution)/shard_map/ppermute | solution.py:246
  14.7 36.0 %copy-start.4 = (bf16[2,512,512]{2,1,0:T(8,128)(2,1)}, bf16[2,512,512]{2,1,0:T(8,128)(2,1)S(1)}, u32[]{:S(2)}) copy-start(bf16[2,512,512]{2,1,0:T(8,128)(2,1)S(1)} %maximum_select_fusion.1) | copy-start | bytes 3145732
  14.7 34.4 %collective-permute-start.3 = (bf16[2,512,512]{2,1,0:T(8,128)(2,1)S(1)}, bf16[2,512,512]{2,1,0:T(8,128)(2,1)}, u32[]{:S(2)}, u32[]{:S(2)}) collective-permute-start(bf16[2,512,512]{2,1,0:T(8,128)(2,1)S(1)} %maximum_select_fusion.1), channel_id=1, source_target_pairs={{0,32},{16,112},{32,64},{48,16},{64,96},{80,48},{96,0},{112,80},{1... | collective-permute-start | bytes 3145736 | tf_op jit(solution)/shard_map/ppermute | solution.py:250
  15.8 48.7 %all-to-all-start = ((bf16[16,64,512]{2,1,0:T(8,128)(2,1)}), bf16[16,64,512]{2,1,0:T(8,128)(2,1)S(1)}, u32[]{:S(2)}, u32[]{:S(2)}) async-start(bf16[16,64,512]{2,1,0:T(8,128)(2,1)} %bitcast.34), calls=%async_computation | async-start | bytes 2097152 | tf_op jit(solution)/shard_map/all_to_all | solution.py:269
  24.0 126.1 %all-gather.4.cloned.1.call-start = ((), (), s32[]{:S(2)}) async-start(), calls=%async_computation.1 | async-start | bytes 4718592 | tf_op jit(solution)/shard_map/all_gather | solution.py:295
  24.0 24.3 %collective-permute-start = (bf16[512,512]{1,0:T(8,128)(2,1)S(1)}, bf16[512,512]{1,0:T(8,128)(2,1)S(1)}, u32[]{:S(2)}, u32[]{:S(2)}) collective-permute-start(bf16[512,512]{1,0:T(8,128)(2,1)S(1)} %copy-done.3), channel_id=1, source_target_pairs={{0,1},{1,2},{2,3},{3,0},{4,5},{5,6},{6,7},{7,4},{8,9},{9,10},{10,1... | collective-permute-start | bytes 1572872 | tf_op jit(solution)/shard_map/ppermute | solution.py:23
  25.4 23.6 %collective-permute-start.1 = (bf16[512,512]{1,0:T(8,128)(2,1)S(1)}, bf16[512,512]{1,0:T(8,128)(2,1)S(1)}, u32[]{:S(2)}, u32[]{:S(2)}) collective-permute-start(bf16[512,512]{1,0:T(8,128)(2,1)S(1)} %copy-done.3), channel_id=1, source_target_pairs={{0,3},{1,0},{2,1},{3,2},{4,7},{5,4},{6,5},{7,6},{8,11},{9,8},{10,9... | collective-permute-start | bytes 1572872 | tf_op jit(solution)/shard_map/ppermute | solution.py:23
  49.1 15.4 %collective-permute-start.7 = (bf16[2,512,512]{2,1,0:T(8,128)(2,1)}, bf16[2,512,512]{2,1,0:T(8,128)(2,1)}, u32[]{:S(2)}, u32[]{:S(2)}) collective-permute-start(bf16[2,512,512]{2,1,0:T(8,128)(2,1)} %collective-permute-done.3), channel_id=1, source_target_pairs={{0,16},{16,0},{1,17},{17,1},{2,18},{18,2},{3,19},{19,3},{4,20},{20... | collective-permute-start | bytes 3145736 | tf_op jit(solution)/shard_map/ppermute | solution.py:246
  50.6 13.9 %collective-permute-start.6 = (bf16[512,512]{1,0:T(8,128)(2,1)S(1)}, bf16[512,512]{1,0:T(8,128)(2,1)}, u32[]{:S(2)}, u32[]{:S(2)}) collective-permute-start(bf16[512,512]{1,0:T(8,128)(2,1)S(1)} %select_bitcast_fusion.1), channel_id=1, source_target_pairs={{0,32},{16,112},{32,64},{48,16},{64,96},{80,48},{96,0},{112,80},{1... | collective-permute-start | bytes 1572872 | tf_op jit(solution)/shard_map/ppermute | solution.py:250
  50.7 9.0 %collective-permute-start.4 = (bf16[256,512]{1,0:T(8,128)(2,1)S(1)}, bf16[256,512]{1,0:T(8,128)(2,1)S(1)}, u32[]{:S(2)}, u32[]{:S(2)}) collective-permute-start(bf16[256,512]{1,0:T(8,128)(2,1)S(1)} %slice.24), channel_id=1, source_target_pairs={{0,1},{1,2},{2,3},{3,0},{4,5},{5,6},{6,7},{7,4},{8,9},{9,10},{10,1... | collective-permute-start | bytes 786440 | tf_op jit(solution)/shard_map/ppermute | solution.py:23
  50.8 8.9 %collective-permute-start.5 = (bf16[256,512]{1,0:T(8,128)(2,1)S(1)}, bf16[256,512]{1,0:T(8,128)(2,1)S(1)}, u32[]{:S(2)}, u32[]{:S(2)}) collective-permute-start(bf16[256,512]{1,0:T(8,128)(2,1)S(1)} %slice.25), channel_id=1, source_target_pairs={{0,3},{1,0},{2,1},{3,2},{4,7},{5,4},{6,5},{7,6},{8,11},{9,8},{10,9... | collective-permute-start | bytes 786440 | tf_op jit(solution)/shard_map/ppermute | solution.py:23
  64.5 2.7 %collective-permute-start.8 = (bf16[16,64,512]{2,1,0:T(8,128)(2,1)S(1)}, bf16[16,64,512]{2,1,0:T(8,128)(2,1)S(1)}, u32[]{:S(2)}, u32[]{:S(2)}) collective-permute-start(bf16[16,64,512]{2,1,0:T(8,128)(2,1)S(1)} %all-to-all-done), channel_id=1, source_target_pairs={{0,16},{16,0},{1,17},{17,1},{2,18},{18,2},{3,19},{19,3},{4,20},{20... | collective-permute-start | bytes 3145736 | tf_op jit(solution)/shard_map/ppermute | solution.py:246
  67.5 25.4 %collective-permute-start.9 = (bf16[2,16,64,512]{3,2,1,0:T(8,128)(2,1)S(1)}, bf16[2,16,64,512]{3,2,1,0:T(8,128)(2,1)}, u32[]{:S(2)}, u32[]{:S(2)}) collective-permute-start(bf16[2,16,64,512]{3,2,1,0:T(8,128)(2,1)S(1)} %maximum_select_fusion.refs_4_.refs_3_.refs_2_), channel_id=1, source_target_pairs={{0,32},{16,112},{32,64},{48,16},{64,96},{80,48},{96,0},{112,80},{1... | collective-permute-start | bytes 6291464 | tf_op jit(solution)/shard_map/ppermute | solution.py:250
  67.6 2.4 %collective-permute-start.10 = (bf16[512,512]{1,0:T(8,128)(2,1)}, bf16[512,512]{1,0:T(8,128)(2,1)S(1)}, u32[]{:S(2)}, u32[]{:S(2)}) collective-permute-start(bf16[512,512]{1,0:T(8,128)(2,1)} %collective-permute-done.6.g2), channel_id=1, source_target_pairs={{0,16},{16,0},{1,17},{17,1},{2,18},{18,2},{3,19},{19,3},{4,20},{20... | collective-permute-start | bytes 1572872 | tf_op jit(solution)/shard_map/ppermute | solution.py:246
  92.8 27.0 %copy-start.14 = (s32[4]{0:T(128)S(1)}, s32[4]{0:T(128)}, u32[]{:S(2)}) copy-start(s32[4]{0:T(128)} %constant.79.clone) | copy-start | bytes 52
  92.8 27.1 %copy-start.12 = (s32[128]{0:T(128)S(1)}, s32[128]{0:T(128)}, u32[]{:S(2)}) copy-start(s32[128]{0:T(128)} %vir.5) | copy-start | bytes 1540
  94.6 14.8 %collective-permute-start.14 = (bf16[16,64,512]{2,1,0:T(8,128)(2,1)S(1)}, bf16[16,64,512]{2,1,0:T(8,128)(2,1)S(1)}, u32[]{:S(2)}, u32[]{:S(2)}) collective-permute-start(bf16[16,64,512]{2,1,0:T(8,128)(2,1)S(1)} %select_bitcast_fusion), channel_id=1, source_target_pairs={{0,32},{16,112},{32,64},{48,16},{64,96},{80,48},{96,0},{112,80},{1... | collective-permute-start | bytes 3145736 | tf_op jit(solution)/shard_map/ppermute | solution.py:250
  95.6 27.5 %collective-permute-start.13 = (bf16[2,16,64,512]{3,2,1,0:T(8,128)(2,1)}, bf16[2,16,64,512]{3,2,1,0:T(8,128)(2,1)S(1)}, u32[]{:S(2)}, u32[]{:S(2)}) collective-permute-start(bf16[2,16,64,512]{3,2,1,0:T(8,128)(2,1)} %collective-permute-done.9.refs_5_.refs_4_.refs_3_), channel_id=1, source_target_pairs={{0,16},{16,0},{1,17},{17,1},{2,18},{18,2},{3,19},{19,3},{4,20},{20... | collective-permute-start | bytes 6291464 | tf_op jit(solution)/shard_map/ppermute | solution.py:246
  97.4 37.5 %collective-permute-start.11 = (bf16[3,512,512]{2,1,0:T(8,128)(2,1)}, bf16[3,512,512]{2,1,0:T(8,128)(2,1)}, u32[]{:S(2)}, u32[]{:S(2)}) collective-permute-start(bf16[3,512,512]{2,1,0:T(8,128)(2,1)} %pick.2.refs_0_), channel_id=1, source_target_pairs={{0,1},{1,2},{2,3},{3,0},{4,5},{5,6},{6,7},{7,4},{8,9},{9,10},{10,1... | collective-permute-start | bytes 4718600 | tf_op jit(solution)/shard_map/ppermute | solution.py:23
  97.7 37.2 %collective-permute-start.12 = (bf16[3,512,512]{2,1,0:T(8,128)(2,1)}, bf16[3,512,512]{2,1,0:T(8,128)(2,1)}, u32[]{:S(2)}, u32[]{:S(2)}) collective-permute-start(bf16[3,512,512]{2,1,0:T(8,128)(2,1)} %pick.2.refs_0_), channel_id=1, source_target_pairs={{0,3},{1,0},{2,1},{3,2},{4,7},{5,4},{6,5},{7,6},{8,11},{9,8},{10,9... | collective-permute-start | bytes 4718600 | tf_op jit(solution)/shard_map/ppermute | solution.py:23
  109.3 13.8 %collective-permute-start.15 = (bf16[16,64,512]{2,1,0:T(8,128)(2,1)S(1)}, bf16[16,64,512]{2,1,0:T(8,128)(2,1)}, u32[]{:S(2)}, u32[]{:S(2)}) collective-permute-start(bf16[16,64,512]{2,1,0:T(8,128)(2,1)S(1)} %collective-permute-done.14.refs_7_.refs_6_.refs_5_), channel_id=1, source_target_pairs={{0,16},{16,0},{1,17},{17,1},{2,18},{18,2},{3,19},{19,3},{4,20},{20... | collective-permute-start | bytes 3145736 | tf_op jit(solution)/shard_map/ppermute | solution.py:246
  136.0 21.5 %collective-permute-start.16 = (bf16[3,256,512]{2,1,0:T(8,128)(2,1)S(1)}, bf16[3,256,512]{2,1,0:T(8,128)(2,1)S(1)}, u32[]{:S(2)}, u32[]{:S(2)}) collective-permute-start(bf16[3,256,512]{2,1,0:T(8,128)(2,1)S(1)} %slice.30), channel_id=1, source_target_pairs={{0,1},{1,2},{2,3},{3,0},{4,5},{5,6},{6,7},{7,4},{8,9},{9,10},{10,1... | collective-permute-start | bytes 2359304 | tf_op jit(solution)/shard_map/ppermute | solution.py:23
  137.3 20.2 %collective-permute-start.17 = (bf16[3,256,512]{2,1,0:T(8,128)(2,1)S(1)}, bf16[3,256,512]{2,1,0:T(8,128)(2,1)S(1)}, u32[]{:S(2)}, u32[]{:S(2)}) collective-permute-start(bf16[3,256,512]{2,1,0:T(8,128)(2,1)S(1)} %slice.31), channel_id=1, source_target_pairs={{0,3},{1,0},{2,1},{3,2},{4,7},{5,4},{6,5},{7,6},{8,11},{9,8},{10,9... | collective-permute-start | bytes 2359304 | tf_op jit(solution)/shard_map/ppermute | solution.py:23
  (12 other events, 79.6 us)
Sparse Core Ops, SparseCore 0:
  9.1 77.6 all-gather.5
  93.0 38.2 all-gather.3

commit v4 on v3

--- a/solution.py
+++ b/solution.py
@@ -167,17 +167,20 @@
             rows = pl.ds(pl.multiple_of(k * n + s * TILE, TILE), TILE)
             masked[rows, :] = v[b] * mask_of(qlab[...], label(s))
 
-    @pl.when(j == 0)
-    def _():
-        total[...] = acc[...]
-
     if split:
-        for i, ta in enumerate(tas):
-            rows = pl.ds(i * (n // 2), n // 2)
-            total[rows, :] += jnp.dot(ta[0], masked[...], preferred_element_type=F32)
+        parts = [jnp.dot(ta[0], masked[...], preferred_element_type=F32) for ta in tas]
+        part = jnp.concatenate(parts, axis=0)
     else:
         blocks = jnp.concatenate([ta[0] for ta in tas], axis=1)
-        total[...] += jnp.dot(blocks, masked[...], preferred_element_type=F32)
+        part = jnp.dot(blocks, masked[...], preferred_element_type=F32)
+
+    @pl.when(j == 0)
+    def _():
+        total[...] = acc[...] + part
+
+    @pl.when(j > 0)
+    def _():
+        total[...] += part
 
     if last:
 

time: 172 us -> 172 us (level)
  no operation moved by 1% of the time
where the time goes in v4:
time: 172 us
  waiting for transfers between devices  59.9 us (35%)
  Pallas kernels  41.8 us (24%)
  starting transfers between devices  38.1 us (22%)
  between operations  13.6 us (8%)
  local copies, waits for them, and re-layouts  10.8 us (6%)
  other arithmetic  7.57 us (4%)
    ppermute x8, waiting for transfers between devices, shift(): return lax.ppermute(a, axis, ring(n, d))  33.2 us
    pallas_call x3, Pallas kernels, particle_part(): pl.pallas_call(functools.partial(particle_kernel, count=count, split=spli...  20.4 us
    ppermute x6, starting transfers between devices, swap(): return lax.ppermute(a, 'c', ring(NC, 1))  16.5 us
    ppermute x8, starting transfers between devices, shift(): return lax.ppermute(a, axis, ring(n, d))  11.1 us
    ppermute x4, waiting for transfers between devices, around(): return lax.ppermute(a, YC, AROUND)  9.39 us
    all_to_all x1, starting transfers between devices, per_device(): v_own = lax.all_to_all(v_rows, VIR, 0, 0, tiled=True)  8.18 us
    pallas_call x1, Pallas kernels, hole_part(): pl.pallas_call(functools.partial(hole_kernel, has_acc=acc is not None), o...  8 us
    all_gather x1, waiting for transfers between devices, per_device(): zag = lax.all_gather(t, z)  7.99 us
  transfers between devices with their start and end apart: 21, of which 10 were waited for; matrix products, arithmetic and copies ran while one was open for 9% of the time, Pallas kernels for 21%

profile of v4, /device:TPU:1, one launch (start us, length us, event | category | flops | bytes accessed | tf_op | source)
XLA Modules:
  0.0 171.8 jit_solution(10380669244450796906)
XLA Ops:
  9.7 3.2 %collective-permute-start.2 = (bf16[512,512]{1,0:T(8,128)(2,1)S(1)}, bf16[512,512]{1,0:T(8,128)(2,1)S(1)}, u32[]{:S(2)}, u32[]{:S(2)}) collective-permute-start(bf16[512,512]{1,0:T(8,128)(2,1)S(1)} %copy-done.3), channel_id=1, source_target_pairs={{0,16},{16,0},{1,17},{17,1},{2,18},{18,2},{3,19},{19,3},{4,20},{20... | collective-permute-start | bytes 1572872 | tf_op jit(solution)/shard_map/ppermute | solution.py:249
  13.0 1.5 collective-permute-done.2
  15.8 8.2 %all-to-all-start = ((bf16[16,64,512]{2,1,0:T(8,128)(2,1)}), bf16[16,64,512]{2,1,0:T(8,128)(2,1)S(1)}, u32[]{:S(2)}, u32[]{:S(2)}) async-start(bf16[16,64,512]{2,1,0:T(8,128)(2,1)} %bitcast.34), calls=%async_computation | async-start | bytes 2097152 | tf_op jit(solution)/shard_map/all_to_all | solution.py:272
  26.8 21.6 %collective-permute-done = bf16[512,512]{1,0:T(8,128)(2,1)S(1)} collective-permute-done((bf16[512,512]{1,0:T(8,128)(2,1)S(1)}, bf16[512,512]{1,0:T(8,128)(2,1)S(1)}, u32[]{:S(2)}, u32[]{:S(2)}) %collective-permute-start) | collective-permute-done | bytes 524320 | tf_op jit(solution)/shard_map/ppermute | solution.py:23
  50.8 2.7 %collective-permute-start.5 = (bf16[256,512]{1,0:T(8,128)(2,1)S(1)}, bf16[256,512]{1,0:T(8,128)(2,1)S(1)}, u32[]{:S(2)}, u32[]{:S(2)}) collective-permute-start(bf16[256,512]{1,0:T(8,128)(2,1)S(1)} %slice.25), channel_id=1, source_target_pairs={{0,3},{1,0},{2,1},{3,2},{4,7},{5,4},{6,5},{7,6},{8,11},{9,8},{10,9... | collective-permute-start | bytes 786440 | tf_op jit(solution)/shard_map/ppermute | solution.py:23
  53.6 6.2 %collective-permute-done.4 = bf16[256,512]{1,0:T(8,128)(2,1)S(1)} collective-permute-done((bf16[256,512]{1,0:T(8,128)(2,1)S(1)}, bf16[256,512]{1,0:T(8,128)(2,1)S(1)}, u32[]{:S(2)}, u32[]{:S(2)}) %collective-permute-start.4) | collective-permute-done | bytes 262176 | tf_op jit(solution)/shard_map/ppermute | solution.py:23
  59.7 4.7 %all-to-all-done = bf16[16,64,512]{2,1,0:T(8,128)(2,1)S(1)} async-done(((bf16[16,64,512]{2,1,0:T(8,128)(2,1)}), bf16[16,64,512]{2,1,0:T(8,128)(2,1)S(1)}, u32[]{:S(2)}, u32[]{:S(2)}) %all-to-all-start) | async-done | bytes 1048608 | tf_op jit(solution)/shard_map/all_to_all | solution.py:272
  64.9 2.3 %collective-permute-done.8 = bf16[16,64,512]{2,1,0:T(8,128)(2,1)S(1)} collective-permute-done((bf16[16,64,512]{2,1,0:T(8,128)(2,1)S(1)}, bf16[16,64,512]{2,1,0:T(8,128)(2,1)S(1)}, u32[]{:S(2)}, u32[]{:S(2)}) %collective-permute-start.8) | collective-permute-done | bytes 1048608 | tf_op jit(solution)/shard_map/ppermute | solution.py:249
  70.8 8.0 %hole_part.1.refs_9_ = f32[512,512]{1,0:T(8,128)} custom-call(s32[6]{0:T(128)} %pad_add_fusion.idx, s32[128]{0:T(128)} %occ.3, s32[1,8192]{1,0:T(1,128)} %broadcast_in_dim_reshape.7.klab, bf16[512,8192]{1,0:T(8,128)(2,1)} %w.3, bf16[1024,512]{1,0:T(8,128)(2,1)} %bitcast.41, bf16[1024,512]{1,0:T(8,128)(2,1)} %bitcast.16.g1, bf16[1024,512]{1,0:T(8,128)(2,1)} %bitcast.17.h1, ...), custom_call_target="tpu_custom_call" | custom-call | flops 2147483648 | bytes 9437184 | tf_op jit(solution)/shard_map/hole_part/pallas_call | solution.py:106
  78.8 8.0 %all-gather.6.cloned.1.call-done = bf16[4096,512]{1,0:T(8,128)(2,1)} async-done(((bf16[512,512]{1,0:T(8,128)(2,1)}), bf16[4096,512]{1,0:T(8,128)(2,1)}) %all-gather.6.cloned.1.call-update) | async-done | bytes 4194320 | tf_op jit(solution)/shard_map/all_gather | solution.py:268
  86.8 4.1 %pick.2.refs_0_ = bf16[3,512,512]{2,1,0:T(8,128)(2,1)} custom-call(s32[3]{0:T(128)} %fusion.1.idx, bf16[8,512,512]{2,1,0:T(8,128)(2,1)} %bitcast.35), custom_call_target="tpu_custom_call" | custom-call | tf_op jit(solution)/shard_map/pick/pallas_call | solution.py:231
  90.9 1.9 %pick.3 = bf16[1,512,512]{2,1,0:T(8,128)(2,1)} custom-call(s32[1]{0:T(128)} %bitcast.6.idx, bf16[8,512,512]{2,1,0:T(8,128)(2,1)} %bitcast.36), custom_call_target="tpu_custom_call" | custom-call | tf_op jit(solution)/shard_map/pick/pallas_call | solution.py:231
  92.9 1.7 select_bitcast_fusion
  95.6 1.7 %collective-permute-start.13 = (bf16[2,16,64,512]{3,2,1,0:T(8,128)(2,1)}, bf16[2,16,64,512]{3,2,1,0:T(8,128)(2,1)S(1)}, u32[]{:S(2)}, u32[]{:S(2)}) collective-permute-start(bf16[2,16,64,512]{3,2,1,0:T(8,128)(2,1)} %collective-permute-done.9.refs_5_.refs_4_.refs_3_), channel_id=1, source_target_pairs={{0,16},{16,0},{1,17},{17,1},{2,18},{18,2},{3,19},{19,3},{4,20},{20... | collective-permute-start | bytes 6291464 | tf_op jit(solution)/shard_map/ppermute | solution.py:249
  97.7 2.4 %collective-permute-start.12 = (bf16[3,512,512]{2,1,0:T(8,128)(2,1)}, bf16[3,512,512]{2,1,0:T(8,128)(2,1)}, u32[]{:S(2)}, u32[]{:S(2)}) collective-permute-start(bf16[3,512,512]{2,1,0:T(8,128)(2,1)} %pick.2.refs_0_), channel_id=1, source_target_pairs={{0,3},{1,0},{2,1},{3,2},{4,7},{5,4},{6,5},{7,6},{8,11},{9,8},{10,9... | collective-permute-start | bytes 4718600 | tf_op jit(solution)/shard_map/ppermute | solution.py:23
  100.1 9.3 %collective-permute-done.14.refs_7_.refs_6_.refs_5_ = bf16[16,64,512]{2,1,0:T(8,128)(2,1)S(1)} collective-permute-done((bf16[16,64,512]{2,1,0:T(8,128)(2,1)S(1)}, bf16[16,64,512]{2,1,0:T(8,128)(2,1)S(1)}, u32[]{:S(2)}, u32[]{:S(2)}) %collective-permute-start.14) | collective-permute-done | bytes 1048608 | tf_op jit(solution)/shard_map/ppermute | solution.py:253
  109.3 10.4 %collective-permute-start.15 = (bf16[16,64,512]{2,1,0:T(8,128)(2,1)S(1)}, bf16[16,64,512]{2,1,0:T(8,128)(2,1)}, u32[]{:S(2)}, u32[]{:S(2)}) collective-permute-start(bf16[16,64,512]{2,1,0:T(8,128)(2,1)S(1)} %collective-permute-done.14.refs_7_.refs_6_.refs_5_), channel_id=1, source_target_pairs={{0,16},{16,0},{1,17},{17,1},{2,18},{18,2},{3,19},{19,3},{4,20},{20... | collective-permute-start | bytes 3145736 | tf_op jit(solution)/shard_map/ppermute | solution.py:249
  121.3 1.8 %maximum_bitcast_fusion.refs_3_ = bf16[1,512,512]{2,1,0:T(8,128)(2,1)} fusion(bf16[256,512]{1,0:T(8,128)(2,1)} %copy-done.10, bf16[256,512]{1,0:T(8,128)(2,1)S(1)} %collective-permute-done.4), kind=kLoop, calls=%fused_computation.4 | loop fusion | flops 1048576 | bytes 1048576 | tf_op jit(solution)/shard_map/broadcast_in_dim | solution.py:305
  124.5 5.7 %particle_part.2.refs_8_ = f32[512,512]{1,0:T(8,128)} custom-call(s32[13]{0:T(128)} %get-tuple-element.42.idx, s32[128]{0:T(128)} %vir.5, s32[1,512]{1,0:T(1,128)} %broadcast_in_dim_reshape.6.qlab, bf16[1,512,512]{2,1,0:T(8,128)(2,1)} %bitcast.37, bf16[1,512,512]{2,1,0:T(8,128)(2,1)} %bitcast.43, bf16[1,512,512]{2,1,0:T(8,128)(2,1)} %bitcast.44, ...), custom_call_target="tpu_custom_call" | custom-call | flops 1073741824 | bytes 5242880 | tf_op jit(solution)/shard_map/particle_part/pallas_call | solution.py:209
  130.1 4.7 %collective-permute-done.11.refs_1_ = bf16[3,512,512]{2,1,0:T(8,128)(2,1)} collective-permute-done((bf16[3,512,512]{2,1,0:T(8,128)(2,1)}, bf16[3,512,512]{2,1,0:T(8,128)(2,1)}, u32[]{:S(2)}, u32[]{:S(2)}) %collective-permute-start.11) | collective-permute-done | bytes 1572896 | tf_op jit(solution)/shard_map/ppermute | solution.py:23
  137.3 2.7 %collective-permute-start.17 = (bf16[3,256,512]{2,1,0:T(8,128)(2,1)S(1)}, bf16[3,256,512]{2,1,0:T(8,128)(2,1)S(1)}, u32[]{:S(2)}, u32[]{:S(2)}) collective-permute-start(bf16[3,256,512]{2,1,0:T(8,128)(2,1)S(1)} %slice.31), channel_id=1, source_target_pairs={{0,3},{1,0},{2,1},{3,2},{4,7},{5,4},{6,5},{7,6},{8,11},{9,8},{10,9... | collective-permute-start | bytes 2359304 | tf_op jit(solution)/shard_map/ppermute | solution.py:23
  141.5 8.5 %particle_part.3.acc = f32[512,512]{1,0:T(8,128)} custom-call(s32[13]{0:T(128)} %get-tuple-element.41.idx, s32[128]{0:T(128)} %vir.5, s32[1,512]{1,0:T(1,128)} %broadcast_in_dim_reshape.6.qlab, bf16[3,512,512]{2,1,0:T(8,128)(2,1)} %pick.2.refs_0_, bf16[3,512,512]{2,1,0:T(8,128)(2,1)} %collective-permute-done.11.refs_1_, ...), custom_call_target="tpu_custom_call" | custom-call | flops 2415919104 | bytes 10485760 | tf_op jit(solution)/shard_map/particle_part/pallas_call | solution.py:209
  150.0 7.5 %far_part.1.refs_7_ = f32[512,512]{1,0:T(8,128)} custom-call(s32[2]{0:T(128)} %pad_add_fusion.1.idx, s32[128]{0:T(128)} %occ.3, s32[1,8192]{1,0:T(1,128)} %broadcast_in_dim_reshape.7.klab, bf16[512,8192]{1,0:T(8,128)(2,1)} %w.3, bf16[4096,512]{1,0:T(8,128)(2,1)} %all-gather.4.cloned.1.call-done.t, f32[512,512]{1,0:T(8,128)} %particle_part.3.acc), custom_call_target="tpu_custom_call" | custom-call | flops 2147483648 | bytes 9437184 | tf_op jit(solution)/shard_map/far_part/pallas_call | solution.py:126
  158.7 6.2 %particle_last.1 = f32[512,512]{1,0:T(8,128)} custom-call(s32[13]{0:T(128)} %get-tuple-element.43.idx, s32[128]{0:T(128)} %vir.5, s32[1,512]{1,0:T(1,128)} %broadcast_in_dim_reshape.6.qlab, bf16[3,256,512]{2,1,0:T(8,128)(2,1)} %copy-done.7, bf16[3,256,512]{2,1,0:T(8,128)(2,1)} %copy-done.8, bf16[2,16,64,512]{3,2,1,0:T(8,128)(2,1)} %copy-done, ...), custom_call_target="tpu_custom_call" | custom-call | flops 805306368 | bytes 4194304 | tf_op jit(solution)/shard_map/particle_last/pallas_call | solution.py:209
  (81 shorter events, 23.2 us)
Async XLA Ops:
  6.5 80.3 %all-gather.6.cloned.1.call-start = ((), (), s32[]{:S(2)}) async-start(), calls=%async_computation.2 | async-start | bytes 4718592 | tf_op jit(solution)/shard_map/all_gather | solution.py:268
  9.7 4.8 %collective-permute-start.2 = (bf16[512,512]{1,0:T(8,128)(2,1)S(1)}, bf16[512,512]{1,0:T(8,128)(2,1)S(1)}, u32[]{:S(2)}, u32[]{:S(2)}) collective-permute-start(bf16[512,512]{1,0:T(8,128)(2,1)S(1)} %copy-done.3), channel_id=1, source_target_pairs={{0,16},{16,0},{1,17},{17,1},{2,18},{18,2},{3,19},{19,3},{4,20},{20... | collective-permute-start | bytes 1572872 | tf_op jit(solution)/shard_map/ppermute | solution.py:249
  14.7 36.0 %copy-start.4 = (bf16[2,512,512]{2,1,0:T(8,128)(2,1)}, bf16[2,512,512]{2,1,0:T(8,128)(2,1)S(1)}, u32[]{:S(2)}) copy-start(bf16[2,512,512]{2,1,0:T(8,128)(2,1)S(1)} %maximum_select_fusion.1) | copy-start | bytes 3145732
  14.7 34.4 %collective-permute-start.3 = (bf16[2,512,512]{2,1,0:T(8,128)(2,1)S(1)}, bf16[2,512,512]{2,1,0:T(8,128)(2,1)}, u32[]{:S(2)}, u32[]{:S(2)}) collective-permute-start(bf16[2,512,512]{2,1,0:T(8,128)(2,1)S(1)} %maximum_select_fusion.1), channel_id=1, source_target_pairs={{0,32},{16,112},{32,64},{48,16},{64,96},{80,48},{96,0},{112,80},{1... | collective-permute-start | bytes 3145736 | tf_op jit(solution)/shard_map/ppermute | solution.py:253
  15.8 48.7 %all-to-all-start = ((bf16[16,64,512]{2,1,0:T(8,128)(2,1)}), bf16[16,64,512]{2,1,0:T(8,128)(2,1)S(1)}, u32[]{:S(2)}, u32[]{:S(2)}) async-start(bf16[16,64,512]{2,1,0:T(8,128)(2,1)} %bitcast.34), calls=%async_computation | async-start | bytes 2097152 | tf_op jit(solution)/shard_map/all_to_all | solution.py:272
  24.0 126.0 %all-gather.4.cloned.1.call-start = ((), (), s32[]{:S(2)}) async-start(), calls=%async_computation.1 | async-start | bytes 4718592 | tf_op jit(solution)/shard_map/all_gather | solution.py:298
  24.0 24.3 %collective-permute-start = (bf16[512,512]{1,0:T(8,128)(2,1)S(1)}, bf16[512,512]{1,0:T(8,128)(2,1)S(1)}, u32[]{:S(2)}, u32[]{:S(2)}) collective-permute-start(bf16[512,512]{1,0:T(8,128)(2,1)S(1)} %copy-done.3), channel_id=1, source_target_pairs={{0,1},{1,2},{2,3},{3,0},{4,5},{5,6},{6,7},{7,4},{8,9},{9,10},{10,1... | collective-permute-start | bytes 1572872 | tf_op jit(solution)/shard_map/ppermute | solution.py:23
  25.4 23.6 %collective-permute-start.1 = (bf16[512,512]{1,0:T(8,128)(2,1)S(1)}, bf16[512,512]{1,0:T(8,128)(2,1)S(1)}, u32[]{:S(2)}, u32[]{:S(2)}) collective-permute-start(bf16[512,512]{1,0:T(8,128)(2,1)S(1)} %copy-done.3), channel_id=1, source_target_pairs={{0,3},{1,0},{2,1},{3,2},{4,7},{5,4},{6,5},{7,6},{8,11},{9,8},{10,9... | collective-permute-start | bytes 1572872 | tf_op jit(solution)/shard_map/ppermute | solution.py:23
  49.1 15.4 %collective-permute-start.7 = (bf16[2,512,512]{2,1,0:T(8,128)(2,1)}, bf16[2,512,512]{2,1,0:T(8,128)(2,1)}, u32[]{:S(2)}, u32[]{:S(2)}) collective-permute-start(bf16[2,512,512]{2,1,0:T(8,128)(2,1)} %collective-permute-done.3), channel_id=1, source_target_pairs={{0,16},{16,0},{1,17},{17,1},{2,18},{18,2},{3,19},{19,3},{4,20},{20... | collective-permute-start | bytes 3145736 | tf_op jit(solution)/shard_map/ppermute | solution.py:249
  50.6 13.9 %collective-permute-start.6 = (bf16[512,512]{1,0:T(8,128)(2,1)S(1)}, bf16[512,512]{1,0:T(8,128)(2,1)}, u32[]{:S(2)}, u32[]{:S(2)}) collective-permute-start(bf16[512,512]{1,0:T(8,128)(2,1)S(1)} %select_bitcast_fusion.1), channel_id=1, source_target_pairs={{0,32},{16,112},{32,64},{48,16},{64,96},{80,48},{96,0},{112,80},{1... | collective-permute-start | bytes 1572872 | tf_op jit(solution)/shard_map/ppermute | solution.py:253
  50.7 9.0 %collective-permute-start.4 = (bf16[256,512]{1,0:T(8,128)(2,1)S(1)}, bf16[256,512]{1,0:T(8,128)(2,1)S(1)}, u32[]{:S(2)}, u32[]{:S(2)}) collective-permute-start(bf16[256,512]{1,0:T(8,128)(2,1)S(1)} %slice.24), channel_id=1, source_target_pairs={{0,1},{1,2},{2,3},{3,0},{4,5},{5,6},{6,7},{7,4},{8,9},{9,10},{10,1... | collective-permute-start | bytes 786440 | tf_op jit(solution)/shard_map/ppermute | solution.py:23
  50.8 8.9 %collective-permute-start.5 = (bf16[256,512]{1,0:T(8,128)(2,1)S(1)}, bf16[256,512]{1,0:T(8,128)(2,1)S(1)}, u32[]{:S(2)}, u32[]{:S(2)}) collective-permute-start(bf16[256,512]{1,0:T(8,128)(2,1)S(1)} %slice.25), channel_id=1, source_target_pairs={{0,3},{1,0},{2,1},{3,2},{4,7},{5,4},{6,5},{7,6},{8,11},{9,8},{10,9... | collective-permute-start | bytes 786440 | tf_op jit(solution)/shard_map/ppermute | solution.py:23
  64.5 2.7 %collective-permute-start.8 = (bf16[16,64,512]{2,1,0:T(8,128)(2,1)S(1)}, bf16[16,64,512]{2,1,0:T(8,128)(2,1)S(1)}, u32[]{:S(2)}, u32[]{:S(2)}) collective-permute-start(bf16[16,64,512]{2,1,0:T(8,128)(2,1)S(1)} %all-to-all-done), channel_id=1, source_target_pairs={{0,16},{16,0},{1,17},{17,1},{2,18},{18,2},{3,19},{19,3},{4,20},{20... | collective-permute-start | bytes 3145736 | tf_op jit(solution)/shard_map/ppermute | solution.py:249
  67.5 25.4 %collective-permute-start.9 = (bf16[2,16,64,512]{3,2,1,0:T(8,128)(2,1)S(1)}, bf16[2,16,64,512]{3,2,1,0:T(8,128)(2,1)}, u32[]{:S(2)}, u32[]{:S(2)}) collective-permute-start(bf16[2,16,64,512]{3,2,1,0:T(8,128)(2,1)S(1)} %maximum_select_fusion.refs_4_.refs_3_.refs_2_), channel_id=1, source_target_pairs={{0,32},{16,112},{32,64},{48,16},{64,96},{80,48},{96,0},{112,80},{1... | collective-permute-start | bytes 6291464 | tf_op jit(solution)/shard_map/ppermute | solution.py:253
  67.6 2.4 %collective-permute-start.10 = (bf16[512,512]{1,0:T(8,128)(2,1)}, bf16[512,512]{1,0:T(8,128)(2,1)S(1)}, u32[]{:S(2)}, u32[]{:S(2)}) collective-permute-start(bf16[512,512]{1,0:T(8,128)(2,1)} %collective-permute-done.6.g2), channel_id=1, source_target_pairs={{0,16},{16,0},{1,17},{17,1},{2,18},{18,2},{3,19},{19,3},{4,20},{20... | collective-permute-start | bytes 1572872 | tf_op jit(solution)/shard_map/ppermute | solution.py:249
  92.8 27.0 %copy-start.14 = (s32[4]{0:T(128)S(1)}, s32[4]{0:T(128)}, u32[]{:S(2)}) copy-start(s32[4]{0:T(128)} %constant.79.clone) | copy-start | bytes 52
  92.8 27.1 %copy-start.12 = (s32[128]{0:T(128)S(1)}, s32[128]{0:T(128)}, u32[]{:S(2)}) copy-start(s32[128]{0:T(128)} %vir.5) | copy-start | bytes 1540
  94.6 14.8 %collective-permute-start.14 = (bf16[16,64,512]{2,1,0:T(8,128)(2,1)S(1)}, bf16[16,64,512]{2,1,0:T(8,128)(2,1)S(1)}, u32[]{:S(2)}, u32[]{:S(2)}) collective-permute-start(bf16[16,64,512]{2,1,0:T(8,128)(2,1)S(1)} %select_bitcast_fusion), channel_id=1, source_target_pairs={{0,32},{16,112},{32,64},{48,16},{64,96},{80,48},{96,0},{112,80},{1... | collective-permute-start | bytes 3145736 | tf_op jit(solution)/shard_map/ppermute | solution.py:253
  95.6 27.5 %collective-permute-start.13 = (bf16[2,16,64,512]{3,2,1,0:T(8,128)(2,1)}, bf16[2,16,64,512]{3,2,1,0:T(8,128)(2,1)S(1)}, u32[]{:S(2)}, u32[]{:S(2)}) collective-permute-start(bf16[2,16,64,512]{3,2,1,0:T(8,128)(2,1)} %collective-permute-done.9.refs_5_.refs_4_.refs_3_), channel_id=1, source_target_pairs={{0,16},{16,0},{1,17},{17,1},{2,18},{18,2},{3,19},{19,3},{4,20},{20... | collective-permute-start | bytes 6291464 | tf_op jit(solution)/shard_map/ppermute | solution.py:249
  97.4 37.5 %collective-permute-start.11 = (bf16[3,512,512]{2,1,0:T(8,128)(2,1)}, bf16[3,512,512]{2,1,0:T(8,128)(2,1)}, u32[]{:S(2)}, u32[]{:S(2)}) collective-permute-start(bf16[3,512,512]{2,1,0:T(8,128)(2,1)} %pick.2.refs_0_), channel_id=1, source_target_pairs={{0,1},{1,2},{2,3},{3,0},{4,5},{5,6},{6,7},{7,4},{8,9},{9,10},{10,1... | collective-permute-start | bytes 4718600 | tf_op jit(solution)/shard_map/ppermute | solution.py:23
  97.7 37.2 %collective-permute-start.12 = (bf16[3,512,512]{2,1,0:T(8,128)(2,1)}, bf16[3,512,512]{2,1,0:T(8,128)(2,1)}, u32[]{:S(2)}, u32[]{:S(2)}) collective-permute-start(bf16[3,512,512]{2,1,0:T(8,128)(2,1)} %pick.2.refs_0_), channel_id=1, source_target_pairs={{0,3},{1,0},{2,1},{3,2},{4,7},{5,4},{6,5},{7,6},{8,11},{9,8},{10,9... | collective-permute-start | bytes 4718600 | tf_op jit(solution)/shard_map/ppermute | solution.py:23
  109.3 13.8 %collective-permute-start.15 = (bf16[16,64,512]{2,1,0:T(8,128)(2,1)S(1)}, bf16[16,64,512]{2,1,0:T(8,128)(2,1)}, u32[]{:S(2)}, u32[]{:S(2)}) collective-permute-start(bf16[16,64,512]{2,1,0:T(8,128)(2,1)S(1)} %collective-permute-done.14.refs_7_.refs_6_.refs_5_), channel_id=1, source_target_pairs={{0,16},{16,0},{1,17},{17,1},{2,18},{18,2},{3,19},{19,3},{4,20},{20... | collective-permute-start | bytes 3145736 | tf_op jit(solution)/shard_map/ppermute | solution.py:249
  136.0 21.5 %collective-permute-start.16 = (bf16[3,256,512]{2,1,0:T(8,128)(2,1)S(1)}, bf16[3,256,512]{2,1,0:T(8,128)(2,1)S(1)}, u32[]{:S(2)}, u32[]{:S(2)}) collective-permute-start(bf16[3,256,512]{2,1,0:T(8,128)(2,1)S(1)} %slice.30), channel_id=1, source_target_pairs={{0,1},{1,2},{2,3},{3,0},{4,5},{5,6},{6,7},{7,4},{8,9},{9,10},{10,1... | collective-permute-start | bytes 2359304 | tf_op jit(solution)/shard_map/ppermute | solution.py:23
  137.3 20.2 %collective-permute-start.17 = (bf16[3,256,512]{2,1,0:T(8,128)(2,1)S(1)}, bf16[3,256,512]{2,1,0:T(8,128)(2,1)S(1)}, u32[]{:S(2)}, u32[]{:S(2)}) collective-permute-start(bf16[3,256,512]{2,1,0:T(8,128)(2,1)S(1)} %slice.31), channel_id=1, source_target_pairs={{0,3},{1,0},{2,1},{3,2},{4,7},{5,4},{6,5},{7,6},{8,11},{9,8},{10,9... | collective-permute-start | bytes 2359304 | tf_op jit(solution)/shard_map/ppermute | solution.py:23
  (12 other events, 79.6 us)
Sparse Core Ops, SparseCore 0:
  9.1 77.6 all-gather.5
  93.0 38.2 all-gather.3
